TPU v7x, 32 devices: a whole 2x2x4 slice. The times are simulated.
32 devices in a mesh: dp: 8 (over z, x), tensor: 4 (over y, core).
Axes of the slice: x: 2, y: 2, z: 4, core: 2. Of those that a mesh axis runs over, the one named last changes fastest.
Arguments:
- input_rows: bfloat16 [32768, 768], P(('dp', 'tensor')), may hold values from -6 to 6
- time_embed: bfloat16 [8, 768], P('dp'), may hold values from -4 to 4
- parents: int32 [8, 13], P('dp'), may hold values from 0 to 11, as said below
- qkv_weight: bfloat16 [768, 3, 768], P('dp', None, 'tensor'), may hold values from -0.21875 to 0.21875
- qv_bias: bfloat16 [2, 768], P(None, 'tensor'), may hold values from -0.59765625 to 0.59765625
- out_weight: bfloat16 [768, 768], P('tensor', 'dp'), may hold values from -3.5 to 3.5
- out_bias: bfloat16 [768], replicated, may hold values from -1.796875 to 1.796875
- inner_weight: bfloat16 [768, 3072], P('dp', 'tensor'), may hold values from -0.21875 to 0.21875
- inner_bias: bfloat16 [3072], P('tensor'), may hold values from -1.796875 to 1.796875
- outer_weight: bfloat16 [3072, 768], P('tensor', 'dp'), may hold values from -0.109375 to 0.109375
- outer_bias: bfloat16 [768], replicated, may hold values from -1.796875 to 1.796875
- norm_gain: bfloat16 [2, 768], replicated, may hold values from 0.5 to 1.5
- norm_shift: bfloat16 [2, 768], replicated, may hold values from -1.796875 to 1.796875
- cotangent: bfloat16 [32768, 768], P(('dp', 'tensor')), may hold values from -6 to 6
Outputs:
- block_out: bfloat16 [32768, 768], P(('dp', 'tensor'))
- input_grad: bfloat16 [32768, 768], P(('dp', 'tensor'))
- qkv_weight_grad: float32 [768, 3, 768], P('dp', None, 'tensor')
- qv_bias_grad: float32 [2, 768], P(None, 'tensor')
- out_weight_grad: float32 [768, 768], P('tensor', 'dp')
- out_bias_grad: float32 [768], replicated
- inner_weight_grad: float32 [768, 3072], P('dp', 'tensor')
- inner_bias_grad: float32 [3072], P('tensor')
- outer_weight_grad: float32 [3072, 768], P('tensor', 'dp')
- outer_bias_grad: float32 [768], replicated
- norm_gain_grad: float32 [2, 768], replicated
- norm_shift_grad: float32 [2, 768], replicated
Inputs may be any that keep to these rules, and one draw needn't show every extreme that they name: `parents`: segment 0 is the trunk, positions 0 to 1023 of a tree, and its entry is 0; segment s >= 1 is block 4 + s - 1, and its entry is smaller than s.
All inputs are finite; a program needn't handle non-finite values.
Results may differ from a plain program's by a relative error of at most 0.02.
Values may be sent and summed in bfloat16 or wider, within the bound.
A program may use at most 256 MiB of HBM per device.

v0:
```python
import functools
import jax, jax.numpy as jnp
from jax import lax
from jax.experimental import pallas as pl
from jax.experimental.pallas import tpu as pltpu
from jax.sharding import PartitionSpec as P
bf = jnp.bfloat16
f32 = jnp.float32
BLK = 256
TRUNK = 1024
NB = 16
HD = 64
HN = 3
SEGS = 13
PAD = 4
LIST = 192
TQ = 512
TK = 1024
FP = 4
BP = 4
BTQ = 1024
BTK = 256
VM = pl.BlockSpec(memory_space=pltpu.VMEM)
SM = pl.BlockSpec(memory_space=pltpu.SMEM)
HB = pl.BlockSpec(memory_space=pltpu.HBM)
NT = (((1,), (1,)), ((), ()))


def mm(a, b, dims=(((1,), (0,)), ((), ()))):
    return lax.dot_general(a, b, dims, preferred_element_type=f32)


def aligned(i, n):
    return pl.ds(pl.multiple_of(i * n, n), n)


def list_pairs(parents, cur, pairs):
    for s in range(1, SEGS):
        cur[s] = jnp.int32(s)

    def level(_, n):
        for s in range(1, SEGS):
            c = cur[s]
            pairs[0, n] = jnp.int32(s + 3)
            pairs[1, n] = c + 3
            cur[s] = jnp.where(c > 0, parents[0, c], 0)
            n = n + jnp.where(c > 0, 1, 0)
        for i in range(PAD - 1):
            pairs[0, n + i] = jnp.int32(NB)
            pairs[1, n + i] = jnp.int32(NB)
        return (n + PAD - 1) // PAD * PAD

    pairs[2, 0] = lax.fori_loop(0, SEGS - 1, level, jnp.int32(0))


PR = 1024


def fwd_kernel(parents, x_hbm, w_hbm, b_ref, qt_hbm, kv_hbm, kt_hbm, o_hbm, mix_hbm, lse_ref, pairs,
               cur, m_s, acc_s, xs, w_s, wt_s, wr_s, br_s, qt_ref, kv_ref, kt_ref, vt_ref, o_ref, mix_ref, sem):
    def fetch(i, slot):
        return pltpu.make_async_copy(x_hbm.at[i], xs.at[slot], sem.at[slot])

    load_w = pltpu.make_async_copy(w_hbm, w_s, sem.at[2])
    load_w.start()
    fetch(0, 0).start()
    list_pairs(parents, cur, pairs)
    load_w.wait()
    bias = b_ref[...].astype(f32)
    bias = jnp.concatenate([bias[0:1], bias[1:2]], 1)
    w = w_s[...].reshape(w_s.shape[0] * w_s.shape[1], w_s.shape[2])
    wt_s[...] = w[:, :HN * HD].T
    for h in range(HN):
        for c in (1, 2):
            to = slice(h * 128 + (c - 1) * HD, h * 128 + c * HD)
            wr_s[:, to] = w[:, c * HN * HD + h * HD:c * HN * HD + (h + 1) * HD]
            part = bias[:, HN * HD + h * HD:HN * HD + (h + 1) * HD] if c == 2 else jnp.zeros((1, HD), f32)
            br_s[:, to] = jnp.broadcast_to(part, (8, HD))
    bias_col = jnp.transpose(jnp.broadcast_to(bias[:, :HN * HD], (8, HN * HD)))
    ones = (lax.broadcasted_iota(jnp.int32, (16, PR), 0) == 0).astype(f32).astype(bf)

    def rows(i, _):
        slot = lax.rem(i, 2)

        @pl.when(i + 1 < NB * BLK // PR)
        def _():
            fetch(i + 1, 1 - slot).start()

        fetch(i, slot).wait()
        cols = aligned(i, PR)
        x = xs[slot]
        kv = (mm(x, wr_s[...]) + br_s[0:1]).astype(bf)
        kv_ref[cols] = kv
        q = (mm(wt_s[...], x, NT) + bias_col[:, 0:1]).astype(bf)
        qt_ref[:, cols] = (q.astype(f32) * 0.125).astype(bf)
        turned = kv.T
        for h in range(HN):
            kt_ref[h * HD:(h + 1) * HD, cols] = turned[h * 128:h * 128 + HD]
            vt_ref[h, :HD, cols] = turned[h * 128 + HD:(h + 1) * 128]
            vt_ref[h, HD:, cols] = ones
        return 0

    lax.fori_loop(0, NB * BLK // PR, rows, 0)
    saves = [pltpu.make_async_copy(a, b, sem.at[3 + n])
             for n, (a, b) in enumerate(((qt_ref, qt_hbm), (kv_ref, kv_hbm), (kt_ref, kt_hbm)))]
    for c in saves:
        c.start()
    zero = jnp.zeros((HD, TQ), bf)

    def tile(i, _):
        qz = [jnp.concatenate([qt_ref[h * HD:(h + 1) * HD, aligned(i, TQ)], zero], 0) for h in range(HN)]
        m, acc = [None] * HN, [None] * HN
        for c in range(TRUNK // TK):
            ks = slice(c * TK, (c + 1) * TK)
            s = [mm(kv_ref[ks, h * 128:(h + 1) * 128], qz[h]) for h in range(HN)]
            new = [jnp.max(x, axis=0, keepdims=True) for x in s]
            if c:
                new = [jnp.maximum(x, y) for x, y in zip(m, new)]
            p = [jnp.exp(x - y).astype(bf) for x, y in zip(s, new)]
            a = [mm(vt_ref[h, :, ks], p[h]) for h in range(HN)]
            if c:
                a = [x * jnp.exp(y - z) + w for x, y, z, w in zip(acc, m, new, a)]
            m, acc = new, a
        for h in range(HN):
            for j in range(TQ // BLK):
                acc_s[i * (TQ // BLK) + j, h] = acc[h][:, j * BLK:(j + 1) * BLK]
                m_s[i * (TQ // BLK) + j, h:h + 1] = m[h][:, j * BLK:(j + 1) * BLK]
        return 0

    lax.fori_loop(0, NB * BLK // TQ, tile, 0)

    def step(g, _):
        work = []
        for p in range(FP):
            q, kb = pairs[0, g * FP + p], jnp.minimum(pairs[1, g * FP + p], NB - 1)
            work += [(q, aligned(jnp.minimum(q, NB - 1), BLK), aligned(kb, BLK), h) for h in range(HN)]
        s = [mm(kv_ref[ks, h * 128:(h + 1) * 128],
                jnp.concatenate([qt_ref[h * HD:(h + 1) * HD, qs], zero[:, :BLK]], 0)) for q, qs, ks, h in work]
        m = [m_s[q, h:h + 1] for q, qs, ks, h in work]
        new = [jnp.maximum(y, jnp.max(x, axis=0, keepdims=True)) for x, y in zip(s, m)]
        p = [jnp.exp(x - y).astype(bf) for x, y in zip(s, new)]
        a = [mm(vt_ref[h, :, ks], x) for x, (q, qs, ks, h) in zip(p, work)]
        a = [acc_s[q, h] * jnp.exp(x - y) + z for x, y, z, (q, qs, ks, h) in zip(m, new, a, work)]
        for x, y, (q, qs, ks, h) in zip(new, a, work):
            m_s[q, h:h + 1] = x
            acc_s[q, h] = y
        return 0

    lax.fori_loop(0, pairs[2, 0] // FP, step, 0)

    rank = lax.axis_index("tensor")

    def finish(i, _):
        qs = aligned(i, BLK)
        slot = jnp.bitwise_xor(rank, i // 4)
        for h in range(HN):
            total = acc_s[i, h, HD:HD + 1, :]
            out = acc_s[i, h, 0:HD, :] / total
            o_ref[h * HD:(h + 1) * HD, qs] = out
            mix_ref[slot, h * HD:(h + 1) * HD, aligned(lax.rem(i, 4), BLK)] = out.astype(bf)
            lse_ref[h:h + 1, qs] = m_s[i, h:h + 1] + jnp.log(total)
        return 0

    lax.fori_loop(0, NB, finish, 0)
    saves += [pltpu.make_async_copy(mix_ref, mix_hbm, sem.at[6]), pltpu.make_async_copy(o_ref, o_hbm, sem.at[7])]
    for c in saves[3:]:
        c.start()
    for c in saves:
        c.wait()


def attn_fwd(parents, whole, w, bias):
    S = NB * BLK
    sd = jax.ShapeDtypeStruct
    vm = pltpu.VMEM
    n = HN * HD
    d = whole.shape[2]
    return pl.pallas_call(
        fwd_kernel,
        out_shape=(sd((n, S), bf), sd((S, 2 * n), bf), sd((n, S), bf), sd((n, S), f32), sd((4, n, S // 4), bf),
                   sd((8, S), f32), sd((3, LIST), jnp.int32)),
        in_specs=[SM, HB, HB, VM], out_specs=(HB,) * 5 + (VM, SM),
        scratch_shapes=[pltpu.SMEM((16,), jnp.int32), vm((NB + 1, 8, BLK), f32), vm((NB + 1, HN, 80, BLK), f32),
                        vm((2, PR, d), bf), vm(w.shape, bf), vm((n, d), bf), vm((d, 2 * n), bf), vm((8, 2 * n), f32),
                        vm((n, S), bf), vm((S, 2 * n), bf), vm((n, S), bf), vm((HN, 80, S), bf),
                        vm((n, S), f32), vm((4, n, S // 4), bf), pltpu.SemaphoreType.DMA((8,))],
        compiler_params=pltpu.CompilerParams(vmem_limit_bytes=63 << 20),
        cost_estimate=pl.CostEstimate(flops=40_000_000_000, bytes_accessed=12_000_000, transcendentals=18_000_000),
        name="tree_attention",
    )(parents, whole, w, bias)


def bwd_kernel(heads, pairs, qt_hbm, kv_hbm, kt_hbm, dots_hbm, o_hbm, lse_ref, rows_in, dqt_hbm, dkv_hbm, rows_out,
               rows_s, dkv_s, dq_s, st_s, dot_ref, qt_ref, kv_ref, kt_ref, dots, o_ref, dqt_ref, dkv_ref, sem):
    loads = [pltpu.make_async_copy(a, b, sem.at[n]) for n, (a, b) in enumerate((
        (dots_hbm, dots), (o_hbm, o_ref), (qt_hbm, qt_ref), (kv_hbm, kv_ref), (kt_hbm, kt_ref)))]
    for c in loads:
        c.start()
    through = [pltpu.make_async_copy(rows_in, rows_s, sem.at[7]), pltpu.make_async_copy(rows_s, rows_out, sem.at[8])]
    through[0].start()
    dkv_s[...] = jnp.zeros_like(dkv_s)
    dq_s[...] = jnp.zeros_like(dq_s)
    rank = lax.axis_index("tensor")
    loads[0].wait()
    for m in range(4):
        dot_ref[:, aligned(jnp.bitwise_xor(rank, m), NB * BLK // 4)] = dots[m]
    loads[1].wait()

    def stats(i, _):
        qs = aligned(i, BLK)
        for n, h in enumerate(heads):
            rows = slice(h * HD, (h + 1) * HD)
            st_s[i, n:n + 1] = jnp.sum(dot_ref[rows, qs].astype(f32) * o_ref[rows, qs], axis=0, keepdims=True)
            st_s[i, 4 + n:5 + n] = lse_ref[h:h + 1, qs]
        return 0

    lax.fori_loop(0, NB, stats, 0)
    for c in loads[2:]:
        c.wait()
    through[0].wait()
    through[1].start()

    def chains(work, width):
        zero = jnp.zeros((HD, width), bf)
        rows = lambda h: slice(h * HD, (h + 1) * HD)
        qz = [jnp.concatenate([qt_ref[rows(h), qs], zero], 0) for h, qs, ks, lse, delta in work]
        dz = [jnp.concatenate([zero, dot_ref[rows(h), qs]], 0) for h, qs, ks, lse, delta in work]
        kv = [kv_ref[ks, h * 128:(h + 1) * 128] for h, qs, ks, lse, delta in work]
        p = [jnp.exp(mm(x, y) - w[3]) for x, y, w in zip(kv, qz, work)]
        ds = [(x * (mm(y, z) - w[4])).astype(bf) for x, y, z, w in zip(p, kv, dz, work)]
        g = [mm(jnp.concatenate([x, y.astype(bf)], 1), jnp.concatenate([z, u], 1), NT)
             for x, y, z, u in zip(ds, p, qz, dz)]
        return g, [mm(kt_ref[rows(h), ks], x) for x, (h, qs, ks, lse, delta) in zip(ds, work)]

    per = BTQ // BLK

    def tile(i, _):
        row = lambda k: jnp.concatenate([st_s[i * per + j, k:k + 1] for j in range(per)], 1)
        dq = [None] * len(heads)
        for c in range(TRUNK // BTK):
            ks = slice(c * BTK, (c + 1) * BTK)
            g, d = chains([(h, aligned(i, BTQ), ks, row(4 + n), row(n)) for n, h in enumerate(heads)], BTQ)
            for n in range(len(heads)):
                dkv_s[ks, n * 128:(n + 1) * 128] += g[n]
                dq[n] = d[n] if c == 0 else dq[n] + d[n]
        for n in range(len(heads)):
            for j in range(per):
                dq_s[i * per + j, n] += dq[n][:, j * BLK:(j + 1) * BLK]
        return 0

    lax.fori_loop(0, NB * BLK // BTQ, tile, 0)

    def step(s, _):
        work, where = [], []
        for p in range(BP):
            q, kb = pairs[0, s * BP + p], pairs[1, s * BP + p]
            qr = jnp.minimum(q, NB - 1)
            for n, h in enumerate(heads):
                work.append((h, aligned(qr, BLK), aligned(jnp.minimum(kb, NB - 1), BLK),
                             st_s[qr, 4 + n:5 + n], st_s[qr, n:n + 1]))
                where.append((q, kb, n))
        for g, d, (q, kb, n) in zip(*chains(work, BLK), where):
            dkv_s[aligned(kb, BLK), n * 128:(n + 1) * 128] += g
            dq_s[q, n] += d
        return 0

    lax.fori_loop(0, pairs[2, 0] // BP, step, 0)

    def finish(i, _):
        for n in range(len(heads)):
            dqt_ref[n * HD:(n + 1) * HD, aligned(i, BLK)] = (dq_s[i, n] * 0.125).astype(bf)
        dkv_ref[aligned(i, BLK)] = dkv_s[aligned(i, BLK)].astype(bf)
        save(i).start()
        return 0

    def save(i):
        return pltpu.make_async_copy(dkv_ref.at[aligned(i, BLK)], dkv_hbm.at[aligned(i, BLK)], sem.at[9 + i])

    lax.fori_loop(0, NB, finish, 0)
    last = pltpu.make_async_copy(dqt_ref, dqt_hbm, sem.at[5])
    last.start()
    for i in range(NB):
        save(i).wait()
    last.wait()
    through[1].wait()


def attn_bwd(heads, pairs, qt, kv, kt, dots, o, lse, rows):
    S = qt.shape[1]
    sd = jax.ShapeDtypeStruct
    n = len(heads)
    return pl.pallas_call(
        functools.partial(bwd_kernel, heads),
        out_shape=(sd((n * HD, S), bf), sd((S, n * 128), bf), sd(rows.shape, rows.dtype)),
        in_specs=[SM] + [HB] * 5 + [VM, HB], out_specs=(HB, HB, HB),
        scratch_shapes=[pltpu.VMEM(rows.shape, rows.dtype), pltpu.VMEM((S + BLK, n * 128), f32), pltpu.VMEM((NB + 1, n, HD, BLK), f32),
                        pltpu.VMEM((NB, 8, BLK), f32), pltpu.VMEM((HN * HD, S), bf)]
        + [pltpu.VMEM(a.shape, a.dtype) for a in (qt, kv, kt, dots, o)]
        + [pltpu.VMEM((n * HD, S), bf), pltpu.VMEM((S, n * 128), bf), pltpu.SemaphoreType.DMA((9 + NB,))],
        compiler_params=pltpu.CompilerParams(vmem_limit_bytes=63 << 20),
        cost_estimate=pl.CostEstimate(flops=20_000_000_000 * n, bytes_accessed=8_000_000 * n, transcendentals=6_000_000 * n),
        name="tree_attention_grad",
    )(pairs, qt, kv, kt, dots, o, lse, rows)


D = 768
SEQ = 4096
ROWS = SEQ // 4
QW = HN * HD
FQ = 768
AT = FQ
OU = FQ + 256
PK = OU + FQ
MESH = pl.DeviceIdType.MESH
HBM = pl.BlockSpec(memory_space=pl.ANY)
TN = (((0,), (0,)), ((), ()))
epsilon = 1e-05
root_half = 0.7071067811865476
inv_root_tau = 0.3989422804014327


def layer_norm(summed, gain_row, shift_row):
    centre = jnp.mean(summed, axis=-1, keepdims=True)
    offset = summed - centre
    inv_std = lax.rsqrt(jnp.mean(offset * offset, axis=-1, keepdims=True) + epsilon)
    normed = offset * inv_std
    return normed * gain_row + shift_row, normed, inv_std


def norm_back(grad_out, normed, inv_std, gain_row):
    scaled = grad_out * gain_row
    return inv_std * (
        scaled
        - jnp.mean(scaled, axis=-1, keepdims=True)
        - normed * jnp.mean(scaled * normed, axis=-1, keepdims=True)
    )


def gelu_parts(u):
    half = 0.5 * (1.0 + lax.erf(u * root_half))
    return u * half, half + u * inv_root_tau * jnp.exp(-0.5 * u * u)


def partner(x, mask):
    return lax.ppermute(x, "tensor", [(i, i ^ mask) for i in range(4)])


def across_x(x):
    return lax.ppermute(x, "dp", [(i, i ^ 1) for i in range(8)])


def flip1(r):
    return r + 1 - 2 * lax.rem(r, 2)


CH = 4
CROWS = ROWS // CH


def remote(src, dst, s, q, dev):
    return pltpu.make_async_remote_copy(
        src_ref=src, dst_ref=dst, send_sem=s, recv_sem=q, device_id=dev, device_id_type=MESH)


def meet(targets, meanwhile=None):
    barrier = pltpu.get_barrier_semaphore()
    for t in targets:
        pl.semaphore_signal(barrier, inc=1, device_id=t, device_id_type=MESH)
    if meanwhile is not None:
        meanwhile()
    pl.semaphore_wait(barrier, len(targets))


class Sends:
    def __init__(self):
        self.started = []

    def go(self, *args):
        c = remote(*args)
        c.start()
        self.started.append(c)
        return c

    def drain(self):
        for c in self.started:
            c.wait_send()


def gather_kernel(with_w, *refs):
    if with_w:
        (inp, te, wq, w1, w2, w3, bias, whole_hbm, wqg_hbm, gz_hbm, gl_hbm, whole, wqg, gz, bcol,
         ysend, yrecv, csend, crecv, out, zsend, zrecv, xsend, xrecv) = refs
    else:
        inp, te, whole_hbm, whole, ysend, yrecv, csend, crecv, out = refs
    r = lax.axis_index("tensor")
    d = lax.axis_index("dp")
    rc, ry = flip1(r), lax.rem(r + 2, 4)
    core, yy = {"tensor": rc}, {"tensor": ry}
    targets = [core, yy]
    if with_w:
        z, x = d // 2, lax.rem(d, 2)
        xx = {"dp": flip1(d)}
        up, down = {"dp": lax.rem(z + 1, 4) * 2 + x}, {"dp": lax.rem(z + 3, 4) * 2 + x}
        targets += [xx, up, down]

    def prepare():
        shift = te[...].astype(f32)
        whole[r] = (inp[...].astype(f32) + shift).astype(bf)
        if with_w:
            for c in range(3):
                wqg[d, :, c * QW:(c + 1) * QW] = wq[c]

    meet(targets, prepare)
    sends = Sends()
    if with_w:

        def line(a, s, slot, way):
            ref = wqg.at[slot * 2 + x] if a == 0 else gz.at[slot]
            k = 2 * (s - 1) + way
            return remote(ref, ref, zsend.at[a, k], zrecv.at[a, k], (up, down)[way])

        def side(i, slot):
            ref = wqg.at[slot * 2 + x]
            return remote(ref, ref, xsend.at[i], xrecv.at[i], xx)

        def can_send(s, way):
            return jnp.logical_and(z < 3, z - s + 1 >= 0) if way == 0 else jnp.logical_and(z > 0, z + s - 1 <= 3)

        def can_recv(s, way):
            return z - s >= 0 if way == 0 else z + s <= 3

        def own(a):
            for way in (0, 1):
                @pl.when(can_send(1, way))
                def _():
                    line(a, 1, z, way).start()

        own(0)
        side(0, z).start()
    rows = [pl.ds(i * CROWS, CROWS) for i in range(CH)]
    yc = []
    for i in range(CH):
        mine = whole.at[r, rows[i]]
        yc.append(sends.go(mine, mine, ysend.at[i], yrecv.at[i], yy))
    c0 = sends.go(whole.at[r], whole.at[r], csend.at[CH], crecv.at[CH], core)
    if with_w:
        part = wqg.shape[1]
        gz[z, :, 0:FQ] = w1[...]
        gz[z, :, OU:] = w2[...]
        bcol[...] = jnp.transpose(jnp.broadcast_to(bias[...].astype(f32).reshape(1, D), (8, D)))
        fill = OU - AT - QW
        column = bcol[pl.ds(pl.multiple_of(d * part, 32), part), 0:1]
        column = jnp.where(lax.broadcasted_iota(jnp.int32, (part, fill), 1) == 0, column, 0.0)
        gz[z, :, AT:OU] = jnp.concatenate([w3[...].astype(f32).T, column], 1).astype(bf)
        own(1)
        for s in (1, 2, 3):
            for way in (0, 1):
                slot = z - s if way == 0 else z + s

                @pl.when(can_recv(s, way))
                def _():
                    for a in (0, 1):
                        line(a, s, slot, way).wait_recv()
                        if s < 3:
                            @pl.when(can_send(s + 1, way))
                            def _():
                                line(a, s + 1, slot, way).start()
                        if a == 0:
                            side(slot_sem(s, way), slot).start()
    keeps = []

    def keep(src, dst):
        c = pltpu.make_async_copy(src, dst, out.at[len(keeps)])
        c.start()
        keeps.append(c)

    keep(whole.at[r], whole_hbm.at[r])
    cc = []
    for i in range(CH):
        yc[i].wait_recv()
        part = whole.at[ry, rows[i]]
        cc.append(sends.go(part, part, csend.at[i], crecv.at[i], core))
    keep(whole.at[ry], whole_hbm.at[ry])
    c0.wait_recv()
    keep(whole.at[rc], whole_hbm.at[rc])
    for c in cc:
        c.wait_recv()
    rd = 3 - r
    keep(whole.at[rd], whole_hbm.at[rd])
    if with_w:
        keep(gz, gz_hbm)
        keep(gz.at[pl.ds(0, 2)], gl_hbm)
        side(0, z).wait()
        for s in (1, 2, 3):
            for way in (0, 1):
                slot = z - s if way == 0 else z + s

                @pl.when(can_recv(s, way))
                def _():
                    side(slot_sem(s, way), slot).wait()

                @pl.when(can_send(s, way))
                def _():
                    for a in (0, 1):
                        line(a, s, slot_of_send(z, s, way), way).wait_send()
        keep(wqg, wqg_hbm)
    for c in keeps:
        c.wait()
    sends.drain()


def slot_of_send(z, s, way):
    return z - s + 1 if way == 0 else z + s - 1


def slot_sem(s, way):
    return 2 * s - 1 + way


def gather_start(inp, te, *weights):
    with_w = len(weights) > 0
    dma = pltpu.SemaphoreType.DMA
    shapes = [jax.ShapeDtypeStruct((4, ROWS, D), bf)]
    args = [inp, te, *weights]
    scratch = []
    sems = [dma((CH,)), dma((CH,)), dma((CH + 1,)), dma((CH + 1,)), dma((8,))]
    if with_w:
        part = weights[0].shape[1]
        line = jax.ShapeDtypeStruct((4, part, PK), bf)
        shapes += [jax.ShapeDtypeStruct((8, part, 3 * QW), bf), line, jax.ShapeDtypeStruct((2, part, PK), bf)]
        scratch = [pltpu.VMEM((D, 8), f32)]
        sems += [dma((2, 6)), dma((2, 6)), dma((7,)), dma((7,))]
    return pl.pallas_call(
        functools.partial(gather_kernel, with_w),
        out_shape=shapes, in_specs=[VM] * len(args), out_specs=[HB] * len(shapes),
        scratch_shapes=[pltpu.VMEM(a.shape, bf) for a in shapes[:3]] + scratch + sems,
        compiler_params=pltpu.CompilerParams(collective_id=0, has_side_effects=True, vmem_limit_bytes=60 << 20),
        name="gather_start",
    )(*args)


RB = 512
NR = ROWS // RB


def middle_kernel(with_w, *refs):
    if with_w:
        wa, wb, wc, wd = refs[:4]
        step, line_s, xsend, xrecv, wsend, wrecv, ssend, srecv = refs[-8:]
        refs = refs[4:-8]
    else:
        wfull, refs = refs[0], refs[1:]
    (mix_hbm, inp_hbm, te, cot_hbm, ob, fb, ng, ns, block_hbm, grad1_hbm, dots_hbm, p00, p01, p10, p11, sums_o,
     inp, cot, block_out, grad1_o, w, wt_s, mix, mixr, gmix, dots, both, ht, gmt, gat, act, gp, slope_s,
     loc, asend, arecv, bsend, brecv, gsend, grecv) = refs
    r = lax.axis_index("tensor")
    d = lax.axis_index("dp")
    x = lax.rem(d, 2)
    ranks = [r, flip1(r), lax.rem(r + 2, 4), 3 - r]
    devices = [{"tensor": k} for k in ranks]
    xx = {"dp": flip1(d)}
    load = pltpu.make_async_copy(mix_hbm, mix, loc.at[5])
    load.start()
    rows_in = [pltpu.make_async_copy(inp_hbm, inp, loc.at[19]), pltpu.make_async_copy(cot_hbm, cot, loc.at[20])]
    for c in rows_in:
        c.start()
    if with_w:
        z = d // 2
        zdev = [{"dp": lax.rem(z + k, 4) * 2 + x} for k in range(4)]
        meet(devices[1:] + [xx] + zdev[1:])
    else:
        meet(devices[1:])
    sends = Sends()
    core = devices[1]
    load.wait()

    def heads_in(b, m):
        cols = pl.ds(b * RB, RB)
        return remote(mix.at[m, :, cols], mixr.at[m, :, cols], asend.at[b, m], arecv.at[b, m], devices[m])

    def heads_out(b, m):
        cols = aligned(b, RB)
        return remote(gmix.at[m, :, cols], dots.at[m, :, cols], bsend.at[b, m], brecv.at[b, m], devices[m])

    heads = [[heads_in(b, m) for m in (3, 2, 1)] for b in range(NR)]
    for c in heads[0]:
        c.start()
    fill = pltpu.make_async_copy(mix.at[0], mixr.at[0], loc.at[0])
    fill.start()

    def weight_moves(j, relay, hand, place):
        rank, side = lax.axis_index("tensor"), lax.rem(lax.axis_index("dp"), 2)
        span = (pl.ds(0, OU), pl.ds(OU, FQ))[j]
        other = lax.rem(rank + 2, 4)
        four, two, end = pl.ds(0, 4), pl.ds(0, 2), pl.ds(2, 2)
        near = {"tensor": flip1(rank)}
        relay(remote(wc.at[end, :, span], w.at[other, end, side, :, span], xsend.at[j], xrecv.at[j],
                     {"dp": flip1(lax.axis_index("dp"))}))
        pieces = ((wa, rank, four, side), (wb, rank, four, 1 - side), (wc, other, four, side), (wd, other, two, 1 - side))
        for i, (ref, t, zz, at) in enumerate(pieces):
            src, dst = ref.at[:, :, span], w.at[t, zz, at, :, span]
            hand(remote(src, dst, wsend.at[j, i], wrecv.at[j, i], near))
            if place is not None:
                place(pltpu.make_async_copy(src, dst, loc.at[11 + 4 * j + i]))

    def whole_fill(j):
        span = (pl.ds(0, OU), pl.ds(OU, FQ))[j]
        return pltpu.make_async_copy(wfull.at[:, :, :, :, span], w.at[:, :, :, :, span], loc.at[1 + j])

    def weight_tail(j):
        rank, side = lax.axis_index("tensor"), lax.rem(lax.axis_index("dp"), 2)
        tail = w.at[lax.rem(rank + 2, 4), pl.ds(2, 2), 1 - side, :, (pl.ds(0, OU), pl.ds(OU, FQ))[j]]
        return remote(tail, tail, wsend.at[j, 4], wrecv.at[j, 4], {"tensor": flip1(rank)})

    if with_w:
        for j in (0, 1):
            weight_moves(j, lambda c: c.start(), lambda c: c.start(), lambda c: c.start())
    else:
        for j in (0, 1):
            whole_fill(j).start()
    for part in heads[1:]:
        for c in part:
            c.start()
    sums_o[...] = jnp.zeros_like(sums_o)
    out_bias, outer_bias = (v[...].astype(f32).reshape(1, D) for v in (ob, fb))
    gains, shifts = ng[...].astype(f32), ns[...].astype(f32)
    gain1, gain2, shift1, shift2 = gains[0:1], gains[1:2], shifts[0:1], shifts[1:2]
    def weights_here(j):
        if with_w:
            def arrived(c):
                c.wait_recv()
                weight_tail(j).start()

            weight_moves(j, arrived, lambda c: c.wait_recv(), lambda c: c.wait())
            weight_tail(j).wait_recv()
        else:
            whole_fill(j).wait()

    weights_here(0)
    fill.wait()
    for c in rows_in:
        c.wait()
    for t in range(4):
        wt_s[t] = jnp.transpose(w[t, :, :, :, AT:OU].reshape(D, OU - AT))
    bias_in = [wt_s[t, QW:QW + 16].astype(f32)[0:1] for t in range(4)]
    w_in = lambda t: w[t, :, :, :, 0:FQ].reshape(D, FQ)
    w_ou = lambda t: w[t, :, :, :, OU:].reshape(D, FQ)

    def add_sum(i, rows):
        sums_o[i:i + 1] += jnp.sum(rows, axis=0, keepdims=True)

    def block(b, _):
        for i in range(NR):
            @pl.when(b == i)
            def _():
                for c in heads[i]:
                    c.wait_recv()
        rows = aligned(b, RB)
        start = inp[rows].astype(f32) + te[...].astype(f32)
        attn = out_bias
        for m in range(4):
            attn = attn + mm(mixr[m, :, rows], wt_s[ranks[m], :QW], TN)
        hidden, normed1, inv1 = layer_norm(start + attn, gain1, shift1)
        low = hidden.astype(bf)
        ht[:, rows] = low.T
        for t in range(4):
            u = mm(low, w_in(t)) + bias_in[t]
            value, slope = gelu_parts(u)
            act[t, rows] = value.astype(bf)
            slope_s[t] = slope.astype(bf)

        @pl.when(b == 0)
        def _():
            weights_here(1)

        mlp = outer_bias
        for t in range(4):
            mlp = mlp + mm(act[t, rows], w_ou(t), NT)
        final, normed2, inv2 = layer_norm(hidden + mlp, gain2, shift2)
        block_out[rows] = final.astype(bf)
        e = cot[rows].astype(f32)
        add_sum(0, e * normed2)
        add_sum(1, e)
        grad2 = norm_back(e, normed2, inv2, gain2)
        gm = grad2.astype(bf)
        gmt[:, rows] = gm.T
        add_sum(2, gm.astype(f32))
        gin = grad2
        for t in range(4):
            g = (mm(gm, w_ou(t)) * slope_s[t].astype(f32)).astype(bf)
            gp[t, rows] = g
            add_sum(6 + t, g.astype(f32))
            gin = gin + mm(g, w_in(t), NT)
        add_sum(3, gin * normed1)
        add_sum(4, gin)
        grad1 = norm_back(gin, normed1, inv1, gain1)
        grad1_o[rows] = grad1
        ga = grad1.astype(bf)
        gat_rows = ga.T
        gat[:, rows] = gat_rows
        add_sum(5, ga.astype(f32))
        for m in (3, 2, 1):
            gmix[m, :, rows] = mm(wt_s[ranks[m], :QW], gat_rows).astype(bf)
            heads_out(b, m).start()
        dots[0, :, rows] = mm(wt_s[r, :QW], gat_rows).astype(bf)
        return 0

    lax.fori_loop(0, NR, block, 0)

    if with_w:
        for j in (0, 1):
            weight_moves(j, lambda c: c.wait_send(), lambda c: c.wait_send(), None)
            weight_tail(j).wait_send()

    def grads(t, m):
        return (lambda: mm(ht[...], gp[t]), lambda: mm(gmt[...], act[t]), lambda: mm(gat[...], mixr[m], NT))

    cols = (slice(0, FQ), slice(OU, PK), slice(AT, AT + QW))
    blank = jnp.zeros((4, 2, 96, OU - AT - QW), bf)
    cut = lambda g: g.reshape(4, 2, 96, g.shape[1])

    def handing(q):
        return remote(w.at[q], both.at[q], gsend.at[q], grecv.at[q], core)

    hops = []

    def hop(n):
        if not with_w:
            return
        if n:
            hops[-1].wait_recv()
        step[n] = step[n - 1] + step[n + 3] if n else sums_o[...]
        hops.append(sends.go(step.at[n], step.at[n + 4], ssend.at[n], srecv.at[n], (core, devices[2], xx)[n]))

    hop(0)
    saves = [pltpu.make_async_copy(grad1_o, grad1_hbm, loc.at[21]), pltpu.make_async_copy(block_out, block_hbm, loc.at[22])]
    for c in saves:
        c.start()
    for q in (1, 0):
        for c, g in zip(cols, grads(ranks[2 * q + 1], 2 * q + 1)):
            w[q, :, :, :, c] = cut(g().astype(bf))
        w[q, :, :, :, AT + QW:OU] = blank
        handing(q).start()
        hop(2 - q)
    for q in (1, 0):
        mine = grads(ranks[2 * q], 2 * q)
        handing(q).wait_recv()
        for c, g in zip(cols, mine):
            both[q, :, :, :, c] = (both[q, :, :, :, c].astype(f32) + cut(g())).astype(bf)
        for n, side in ((0, x), (1, 1 - x)):
            to = ((p00, p01), (p10, p11))[q][n]
            saves.append(pltpu.make_async_copy(both.at[q, :, side], to, loc.at[6 + 2 * q + n]))
            saves[-1].start()
        if with_w and q:
            hops[-1].wait_recv()
            line_s[z] = step[2] + step[6]
            ends = [sends.go(line_s.at[z], line_s.at[z], ssend.at[2 + k], srecv.at[2 + k], zdev[k]) for k in (1, 2, 3)]
    if with_w:
        for c in ends:
            c.wait_recv()
        sums_o[...] = ((line_s[0] + line_s[1]) + line_s[2]) + line_s[3]
    for b in range(NR):
        for m in (1, 2, 3):
            heads_out(b, m).wait()
        for c in heads[b]:
            c.wait_send()
    saves.append(pltpu.make_async_copy(dots, dots_hbm, loc.at[10]))
    saves[-1].start()
    for c in saves:
        c.wait()
    for q in range(2):
        handing(q).wait_send()
    sends.drain()


def middle(weights, mix, *rest):
    sd = jax.ShapeDtypeStruct
    dma = pltpu.SemaphoreType.DMA
    with_w = len(weights) > 1
    vm = pltpu.VMEM
    tokens = (D, ROWS)
    extra = [vm((7, 16, D), f32), vm((4, 16, D), f32), dma((2,)), dma((2,)), dma((2, 5)), dma((2, 5)),
             dma((6,)), dma((6,))] if with_w else []
    return pl.pallas_call(
        functools.partial(middle_kernel, with_w),
        out_shape=(sd((ROWS, D), bf), sd((ROWS, D), f32), sd((4, QW, ROWS), bf),
                   *([sd((4, 96, PK), bf)] * 4), sd((16, D), f32)),
        in_specs=[HB] * len(weights) + [HB, HB, VM, HB] + [VM] * 4, out_specs=(HB, HB, HB, HB, HB, HB, HB, VM),
        scratch_shapes=[vm((ROWS, D), bf), vm((ROWS, D), bf), vm((ROWS, D), bf), vm((ROWS, D), f32),
                        vm((4, 4, 2, 96, PK), bf), vm((4, OU - AT, D), bf), vm((4, QW, ROWS), bf),
                        vm((4, QW, ROWS), bf), vm((4, QW, ROWS), bf), vm((4, QW, ROWS), bf),
                        vm((2, 4, 2, 96, PK), bf), vm(tokens, bf), vm(tokens, bf), vm(tokens, bf),
                        vm((4, ROWS, FQ), bf), vm((4, ROWS, FQ), bf), vm((4, RB, FQ), bf),
                        dma((23,)), dma((NR, 4)), dma((NR, 4)), dma((NR, 4)), dma((NR, 4)), dma((2,)), dma((2,))] + extra,
        compiler_params=pltpu.CompilerParams(collective_id=2, has_side_effects=True, vmem_limit_bytes=63 << 20),
        cost_estimate=pl.CostEstimate(flops=33_000_000_000, bytes_accessed=50_000_000, transcendentals=9_000_000),
        name="middle",
    )(*weights, mix, *rest)


def final_kernel(with_w, *refs):
    if with_w:
        (x_hbm, w_hbm, dqt_hbm, dkv_hbm, g1_hbm, m0_hbm, m1_hbm, m2_hbm, m3_hbm, out, pair, qo, mo,
         x_s, w_s, wr_s, dqt, dkv, grad1, part, crv, ysd, yrv, m0, m1, m2, m3, zsm, zrm, dwq, xrq, zsq, zrq,
         prv, psd, prs, loc, csend, crecv, ysend, yrecv, xsend, xrecv, zsend, zrecv) = refs
    else:
        (x_hbm, w_hbm, dqt_hbm, dkv_hbm, g1_hbm, out, pair, dw,
         x_s, w_s, wr_s, dqt, dkv, grad1, part, crv, ysd, yrv, loc, csend, crecv, ysend, yrecv) = refs
    pulls = [(w_hbm, w_s), (dqt_hbm, dqt), (dkv_hbm, dkv)]
    pulls += [(m0_hbm, m0), (m1_hbm, m1), (m2_hbm, m2), (m3_hbm, m3)] if with_w else []
    pulls += [(x_hbm, x_s), (g1_hbm, grad1)]
    loads = [pltpu.make_async_copy(a, b, loc.at[n]) for n, (a, b) in enumerate(pulls)]
    for c in loads[:-2]:
        c.start()
    r = lax.axis_index("tensor")
    d = lax.axis_index("dp")
    rc, ry = flip1(r), lax.rem(r + 2, 4)
    rd = 3 - r
    core, yy = {"tensor": rc}, {"tensor": ry}
    targets = [core, yy]
    if with_w:
        z, x = d // 2, lax.rem(d, 2)
        xo = 1 - x
        zs = [lax.rem(z + k, 4) for k in range(4)]
        xx = {"dp": flip1(d)}
        zdev = [{"dp": zs[k] * 2 + x} for k in range(4)]
        targets += [xx] + zdev[1:]
    meet(targets)
    sends = Sends()
    go = sends.go
    wait = lambda *which: [loads[n].wait() for n in which]
    rows = [pl.ds(i * CROWS, CROWS) for i in range(CH)]
    if with_w:
        wait(3, 4, 5, 6)
        zm = []
        for k in (1, 2, 3, 0):
            at = zs[k]
            zsm[k] = ((m0[at].astype(f32) + m1[at].astype(f32)) + (m2[at].astype(f32) + m3[at].astype(f32))).astype(bf)
            if k:
                zm.append(go(zsm.at[k], zrm.at[k - 1], zsend.at[1, k - 1], zrecv.at[1, k - 1], zdev[k]))
    wait(0, 1, 2)
    for c in loads[-2:]:
        c.start()
    w = w_s[...].reshape(D, 3 * QW)
    for h in range(HN):
        for c in (1, 2):
            wr_s[:, h * 128 + (c - 1) * HD:h * 128 + c * HD] = w[:, c * QW + h * HD:c * QW + (h + 1) * HD]
    wqs = w[:, :QW]

    def project_back(t, i):
        at = pl.ds(pl.multiple_of(t * ROWS + i * CROWS, CROWS), CROWS)
        part[t, rows[i]] = (mm(dqt[:, at], wqs, (((0,), (1,)), ((), ()))) + mm(dkv[at], wr_s[...], NT)).astype(bf)

    first, second, third = [], [], []
    for i in range(CH):
        project_back(rd, i)
        second.append(go(part.at[rd, rows[i]], crv.at[1, rows[i]], csend.at[1, i], crecv.at[1, i], core))
        project_back(ry, i)
        if i:
            second[i - 1].wait_recv()
            prev = rows[i - 1]
            ysd[prev] = (part[ry, prev].astype(f32) + crv[1, prev].astype(f32)).astype(bf)
            third.append(go(ysd.at[prev], yrv.at[prev], ysend.at[i - 1], yrecv.at[i - 1], yy))
    prev = rows[CH - 1]
    second[CH - 1].wait_recv()
    ysd[prev] = (part[ry, prev].astype(f32) + crv[1, prev].astype(f32)).astype(bf)
    third.append(go(ysd.at[prev], yrv.at[prev], ysend.at[CH - 1], yrecv.at[CH - 1], yy))

    wait(len(loads) - 2)
    whole = x_s[...].reshape(SEQ, D)
    aq = mm(dqt[...], whole)
    akv = mm(dkv[...], whole, TN)
    blocks = [aq]
    for c in (0, 1):
        blocks += [akv[h * 128 + c * HD:h * 128 + (c + 1) * HD] for h in range(HN)]
    dwt = jnp.concatenate(blocks, 0).T.astype(bf)
    sum_q = jnp.sum(dqt[...].astype(f32), axis=1, keepdims=True)
    sum_q = jnp.transpose(jnp.broadcast_to(sum_q, (QW, 8)))
    sum_kv = jnp.sum(dkv[...].astype(f32), axis=0, keepdims=True)
    sum_v = jnp.concatenate([sum_kv[:, h * 128 + HD:(h + 1) * 128] for h in range(HN)], 1)
    pairs = jnp.concatenate([sum_q[0:1], sum_v, jnp.zeros((6, QW), f32)], 0)
    if with_w:
        dwq[...] = dwt.reshape(dwq.shape)
        xq = go(dwq.at[:, xo], xrq, xsend.at[0], xrecv.at[0], xx)
        prs[...] = pairs
        px = go(prs, prv, xsend.at[1], xrecv.at[1], xx)
    for i in range(CH):
        project_back(rc, i)
        first.append(go(part.at[rc, rows[i]], crv.at[0, rows[i]], csend.at[0, i], crecv.at[0, i], core))
        project_back(r, i)
    if with_w:
        px.wait_recv()
        psd[z] = prs[...] + prv[...]
        zp = [go(psd.at[z], psd.at[z], zsend.at[2, k - 1], zrecv.at[2, k - 1], zdev[k]) for k in (1, 2, 3)]
        xq.wait_recv()
        for k in range(4):
            zsq[k] = (dwq[zs[k], x].astype(f32) + xrq[zs[k]].astype(f32)).astype(bf)
        zq = [go(zsq.at[k], zrq.at[k - 1], zsend.at[0, k - 1], zrecv.at[0, k - 1], zdev[k]) for k in (1, 2, 3)]
    else:
        dw[...] = dwt
        pair[...] = pairs
    wait(len(loads) - 1)
    for i in range(CH):
        first[i].wait_recv()
        third[i].wait_recv()
        out[rows[i]] = (part[r, rows[i]].astype(f32) + crv[0, rows[i]].astype(f32)
                        + yrv[rows[i]].astype(f32) + grad1[rows[i]]).astype(bf)
    if with_w:
        for c in zq:
            c.wait_recv()
        whole_q = (zsq[0].astype(f32) + zrq[0].astype(f32)) + (zrq[1].astype(f32) + zrq[2].astype(f32))
        qo[...] = whole_q
        for c in zp:
            c.wait_recv()
        pair[...] = ((psd[0] + psd[1]) + psd[2]) + psd[3]
        for c in zm:
            c.wait_recv()
        mo[...] = (zsm[0].astype(f32) + zrm[0].astype(f32)) + (zrm[1].astype(f32) + zrm[2].astype(f32))
    sends.drain()


def final(whole, w, dqt, dkv, grad1, *more):
    with_w = len(more) > 0
    dma = pltpu.SemaphoreType.DMA
    sd = jax.ShapeDtypeStruct
    vm = pltpu.VMEM
    rows = (ROWS, D)
    like = lambda a: vm(a.shape, a.dtype)
    shapes = [sd(rows, bf), sd((8, QW), f32)]
    args = [whole, w, dqt, dkv, grad1, *more]
    scratch = [like(whole), like(w), vm((D, 2 * QW), bf), like(dqt), like(dkv), like(grad1), vm((4,) + rows, bf),
               vm((2,) + rows, bf), vm(rows, bf), vm(rows, bf)]
    sems = [dma((9,)), dma((2, CH)), dma((2, CH)), dma((CH,)), dma((CH,))]
    if with_w:
        n = w.shape[1]
        shapes += [sd((n, 3 * QW), f32), sd((n, PK), f32)]
        scratch += [like(m) for m in more] + [vm((4, n, PK), bf), vm((3, n, PK), bf),
                    vm((4, 2, n, 3 * QW), bf), vm((4, n, 3 * QW), bf), vm((4, n, 3 * QW), bf), vm((3, n, 3 * QW), bf),
                    vm((8, QW), f32), vm((4, 8, QW), f32), vm((8, QW), f32)]
        sems += [dma((2,)), dma((2,)), dma((3, 3)), dma((3, 3))]
    else:
        shapes += [sd((D, 3 * QW), bf)]
    return pl.pallas_call(
        functools.partial(final_kernel, with_w),
        out_shape=shapes,
        in_specs=[HB] * len(args), out_specs=[VM] * len(shapes),
        scratch_shapes=scratch + sems,
        compiler_params=pltpu.CompilerParams(
            collective_id=1, has_side_effects=True, vmem_limit_bytes=60 << 20),
        name="final",
    )(*args)


def emit_kernel(*refs):
    sources, outs, kept, sem = refs[:5], refs[5:16], refs[16:21], refs[21]
    loads = [pltpu.make_async_copy(a, b, sem.at[n]) for n, (a, b) in enumerate(zip(sources, kept))]
    for c in loads:
        c.start()
    input_grad, qkv_o, pair_o, out_o, out_b, inner_o, inner_b, outer_o, outer_b, gain_o, shift_o = outs
    save = pltpu.make_async_copy(kept[0], input_grad, sem.at[5])
    loads[0].wait()
    save.start()
    for c in loads[1:]:
        c.wait()
    pair, qkv, share, sums = kept[1:]
    for c in range(3):
        qkv_o[c] = qkv[:, c * QW:(c + 1) * QW]
    pair_o[...] = pair[0:2]
    inner_o[...] = share[:, 0:FQ]
    outer_o[...] = share[:, OU:]
    out_o[...] = share[:, AT:OU].T[:QW]
    out_b[...] = sums[5]
    inner_b[...] = sums[6 + lax.axis_index("tensor")]
    outer_b[...] = sums[2]
    gain_o[...] = jnp.concatenate([sums[3:4], sums[0:1]], 0)
    shift_o[...] = jnp.concatenate([sums[4:5], sums[1:2]], 0)
    save.wait()


def emit(*arrays):
    sd = jax.ShapeDtypeStruct
    n = arrays[3].shape[0]
    rows = sd((ROWS, D), bf)
    vec = sd((D,), f32)
    shapes = (rows, sd((3, n, QW), f32), sd((2, QW), f32), sd((QW, n), f32), vec, sd((n, FQ), f32), vec,
              sd((n, FQ), f32), vec, sd((2, D), f32), sd((2, D), f32))
    return pl.pallas_call(
        emit_kernel, out_shape=shapes, in_specs=[HB] * 5, out_specs=(HB,) + (VM,) * 10,
        scratch_shapes=[pltpu.VMEM(a.shape, a.dtype) for a in arrays] + [pltpu.SemaphoreType.DMA((6,))],
        compiler_params=pltpu.CompilerParams(vmem_limit_bytes=60 << 20),
        name="emit",
    )(*arrays)


def add_low(a, b):
    return (a.astype(f32) + b.astype(f32)).astype(bf)


def on_device(
    ring, input_rows, time_embed, parents, qkv_weight, qv_bias, out_weight, out_bias, inner_weight,
    inner_bias, outer_weight, outer_bias, norm_gain, norm_shift, cotangent,
):
    rank = lax.axis_index("tensor")
    dpos = lax.axis_index("dp")
    part = qkv_weight.shape[0]
    own_ring = ring == 8

    if own_ring:
        whole, w_all, gz, half = gather_start(
            input_rows, time_embed, jnp.transpose(qkv_weight, (1, 0, 2)), inner_weight, outer_weight.T, out_weight,
            inner_bias)
        diagonal = [(i * 4 + j, (i ^ 1) * 4 + (j ^ 2)) for i in range(8) for j in range(4)]
        cross = lambda a: lax.ppermute(a, ("dp", "tensor"), diagonal)
        weights = [gz, across_x(gz), partner(gz, 2), cross(half)]
    else:
        whole = gather_start(input_rows, time_embed)[0]
        w_all = lax.all_gather(qkv_weight.reshape(part, 3 * QW), "dp", axis=0, tiled=True).reshape(8, 96, 3 * QW)
        bias_part = lax.dynamic_slice_in_dim(inner_bias, dpos * part, part, 0)
        packed = jnp.concatenate([inner_weight, out_weight.T, bias_part[:, None],
                                  jnp.zeros((part, OU - AT - QW - 1), bf), outer_weight.T], axis=1)
        packed = lax.all_gather(packed, "dp", axis=0, tiled=True)
        weights = [lax.all_gather(packed, "tensor", axis=0, tiled=False).reshape(4, 4, 2, 96, PK)]

    qt, kv, kt, ot, mix, lse, pairs = attn_fwd(parents, whole, w_all, qv_bias)
    block_out, grad1, dots, *parts, sums = middle(
        weights, mix, input_rows, time_embed, cotangent, out_bias, outer_bias, norm_gain, norm_shift)
    if own_ring:
        parts = [parts[0], across_x(parts[1]), partner(parts[2], 2), cross(parts[3])]
    else:
        far = [partner(parts[2], 2), partner(parts[3], 2)]
    dqt, dkv, block_out = attn_bwd((0, 1, 2), pairs, qt, kv, kt, dots, ot, lse, block_out)
    if own_ring:
        input_grad, pair, qkv_share, share = final(whole, w_all, dqt, dkv, grad1, *parts)
        (input_grad, qkv_share, pair, out_share, out_sum, inner_share, inner_sum, outer_share, outer_sum,
         gains, shifts) = emit(input_grad, pair, qkv_share, share, sums)
        return (block_out, input_grad, jnp.transpose(qkv_share, (1, 0, 2)), pair, out_share, out_sum,
                inner_share, inner_sum, outer_share.T, outer_sum, gains, shifts)
    else:
        input_grad, pair, dwq = final(whole, w_all, dqt, dkv, grad1)
        own, other = add_low(parts[0], far[0]), add_low(parts[1], far[1])
        even = dpos % 2 == 0
        mine = jnp.stack([jnp.where(even, own, other), jnp.where(even, other, own)], axis=1).reshape(D, PK)
        share = lax.psum_scatter(mine, "dp", scatter_dimension=0, tiled=True).astype(f32)
        qkv_share = lax.psum_scatter(dwq, "dp", scatter_dimension=0, tiled=True).astype(f32).reshape(part, 3, QW)
        pair = lax.psum(pair, "dp")
        sums = jnp.sum(lax.all_gather(sums, ("dp", "tensor"), axis=0, tiled=False), axis=0)
    return (
        block_out,
        input_grad,
        qkv_share,
        pair[:2],
        share[:, AT:AT + QW].T,
        sums[5],
        share[:, :FQ],
        lax.dynamic_index_in_dim(sums[6:10], rank, 0, keepdims=False),
        share[:, OU:].T,
        sums[2],
        jnp.stack([sums[3], sums[0]]),
        jnp.stack([sums[4], sums[1]]),
    )


def solution(mesh):
    both = P(("dp", "tensor"), None)
    return jax.shard_map(
        functools.partial(on_device, mesh.shape["dp"]),
        mesh=mesh,
        in_specs=(
            both, P("dp", None), P("dp", None), P("dp", None, "tensor"), P(None, "tensor"),
            P("tensor", "dp"), P(), P("dp", "tensor"), P("tensor"), P("tensor", "dp"), P(), P(), P(), both,
        ),
        out_specs=(
            both, both, P("dp", None, "tensor"), P(None, "tensor"), P("tensor", "dp"), P(),
            P("dp", "tensor"), P("tensor"), P("tensor", "dp"), P(), P(), P(),
        ),
        check_vma=False,
    )
```

profile of v0, /device:TPU:0, one launch (start us, length us, event | category | flops | bytes accessed | tf_op | source)
XLA Modules:
  0.0 285.4 jit_solution(4887907428143838954)
XLA Ops:
  0.6 46.0 %gather_start.1 = (bf16[4,1024,768]{2,1,0:T(8,128)(2,1)}, bf16[8,96,576]{2,1,0:T(8,128)(2,1)}, bf16[4,96,1792]{2,1,0:T(8,128)(2,1)}, bf16[2,96,1792]{2,1,0:T(8,128)(2,1)}) custom-call(bf16[1024,768]{1,0:T(8,128)(2,1)} %refs_5_.3, bf16[1,768]{1,0:T(2,128)(2,1)} %refs_6_.3, bf16[3,96,192]{2,1,0:T(8,128)(2,1)} %bitcast.4, bf16[96,768]{1,0:T(8,128)(2,1)} %refs_3_.1, ...), custom_call_target="tpu_custom_call" | custom-call | tf_op jit(solution)/shard_map/gather_start/pallas_call | solution.py:533
  46.7 0.5 collective-permute-start.1
  47.2 1.5 collective-permute-start
  48.7 1.6 collective-permute-start.2
  50.2 40.6 %tree_attention.1 = (bf16[192,4096]{1,0:T(8,128)(2,1)}, bf16[4096,384]{1,0:T(8,128)(2,1)}, bf16[192,4096]{1,0:T(8,128)(2,1)}, f32[192,4096]{1,0:T(8,128)}, bf16[...) custom-call(s32[1,13]{1,0:T(1,128)} %parents.1, ...), custom_call_target="tpu_custom_call" | custom-call | flops 40000000000 | bytes 12000000 | tf_op jit(solution)/shard_map/tree_attention/pallas_call | solution.py:178
  90.8 4.8 %collective-permute-done.2.refs_3_ = bf16[2,96,1792]{2,1,0:T(8,128)(2,1)S(1)} collective-permute-done((bf16[2,96,1792]{2,1,0:T(8,128)(2,1)}, bf16[2,96,1792]{2,1,0:T(8,128)(2,1)S(1)}, u32[]{:S(2)}, u32[]{:S(2)}) %collective-permute-start.2) | collective-permute-done | bytes 688160 | tf_op jit(solution)/shard_map/ppermute | solution.py:1013
  95.7 0.0 copy-start
  95.7 0.0 collective-permute-done.1.refs_2_
  95.7 0.0 collective-permute-done.refs_1_
  95.7 0.8 copy-done
  96.5 74.9 %middle.1 = (bf16[1024,768]{1,0:T(8,128)(2,1)}, f32[1024,768]{1,0:T(8,128)}, bf16[4,192,1024]{2,1,0:T(8,128)(2,1)}, bf16[4,96,1792]{2,1,0:T(8,128)(2,1)}, bf16[4...) custom-call(bf16[4,96,1792]{2,1,0:T(8,128)(2,1)} %get-tuple-element.55., ...), custom_call_target="tpu_custom_call" | custom-call | flops 32999999488 | bytes 50000000 | tf_op jit(solution)/shard_map/middle/pallas_call | solution.py:784
  171.4 0.6 collective-permute-start.3
  172.0 0.4 collective-permute-start.4
  172.4 2.6 collective-permute-start.5
  175.0 57.9 %tree_attention_grad.1 = (bf16[192,4096]{1,0:T(8,128)(2,1)}, bf16[4096,384]{1,0:T(8,128)(2,1)}, bf16[1024,768]{1,0:T(8,128)(2,1)}) custom-call(s32[3,192]{1,0:T(4,128)} %get-tuple-element.51.pairs, bf16[192,4096]{1,0:T(8,128)(2,1)} %get-tuple-element.52.qt_hbm, bf16[4096,384]{1,0:T(8,128)(2,1)} %get-tuple-element.53.kv_hbm, ...), custom_call_target="tpu_custom_call" | custom-call | flops 60000002048 | bytes 24000000 | tf_op jit(solution)/shard_map/tree_attention_grad/pallas_call | solution.py:292
  232.9 0.0 collective-permute-done.3.refs_6_
  232.9 0.0 collective-permute-done.4.refs_7_
  232.9 0.0 collective-permute-done.5.refs_8_
  232.9 48.4 %final.1 = (bf16[1024,768]{1,0:T(8,128)(2,1)}, f32[8,192]{1,0:T(8,128)}, f32[96,576]{1,0:T(8,128)}, f32[96,1792]{1,0:T(8,128)}) custom-call(bf16[4,1024,768]{2,1,0:T(8,128)(2,1)} %get-tuple-element.49.x_hbm.refs_0_, bf16[8,96,576]{2,1,0:T(8,128)(2,1)} %get-tuple-element.50.w_hbm.refs_1_, bf16[192,4096]{1,0:T(8,128)(2,1)} %get-tuple-element.63.refs_2_, ...), custom_call_target="tpu_custom_call" | custom-call | tf_op jit(solution)/shard_map/final/pallas_call | solution.py:943
  281.3 3.6 %emit.1 = (bf16[1024,768]{1,0:T(8,128)(2,1)}, f32[3,96,192]{2,1,0:T(8,128)}, f32[2,192]{1,0:T(2,128)}, f32[192,96]{1,0:T(8,128)}, f32[768]{0:T(1024)}, /*index=5...) custom-call(bf16[1024,768]{1,0:T(8,128)(2,1)} %get-tuple-element.70., ...), custom_call_target="tpu_custom_call" | custom-call | tf_op jit(solution)/shard_map/emit/pallas_call | solution.py:987
Async XLA Ops:
  46.7 49.0 %collective-permute-start.1 = (bf16[4,96,1792]{2,1,0:T(8,128)(2,1)}, bf16[4,96,1792]{2,1,0:T(8,128)(2,1)}, u32[]{:S(2)}, u32[]{:S(2)}) collective-permute-start(bf16[4,96,1792]{2,1,0:T(8,128)(2,1)} %get-tuple-element.55.refs_0_), channel_id=1, source_target_pairs={{0,2},{1,3},{2,0},{3,1},{4,6},{5,7},{6,4},{7,5},{8,10},{9,11},{10,... | collective-permute-start | bytes 4128776 | tf_op jit(solution)/shard_map/ppermute | solution.py:345
  47.2 48.5 %collective-permute-start = (bf16[4,96,1792]{2,1,0:T(8,128)(2,1)}, bf16[4,96,1792]{2,1,0:T(8,128)(2,1)}, u32[]{:S(2)}, u32[]{:S(2)}) collective-permute-start(bf16[4,96,1792]{2,1,0:T(8,128)(2,1)} %get-tuple-element.55.refs_0_), channel_id=1, source_target_pairs={{0,4},{4,0},{8,12},{12,8},{16,20},{20,16},{24,28},{28,24},{1,5},{5... | collective-permute-start | bytes 4128776 | tf_op jit(solution)/shard_map/ppermute | solution.py:349
  48.7 47.0 %collective-permute-start.2 = (bf16[2,96,1792]{2,1,0:T(8,128)(2,1)}, bf16[2,96,1792]{2,1,0:T(8,128)(2,1)S(1)}, u32[]{:S(2)}, u32[]{:S(2)}) collective-permute-start(bf16[2,96,1792]{2,1,0:T(8,128)(2,1)} %get-tuple-element.56), channel_id=1, source_target_pairs={{0,6},{1,7},{2,4},{3,5},{4,2},{5,3},{6,0},{7,1},{8,14},{9,15},{10,... | collective-permute-start | bytes 2064392 | tf_op jit(solution)/shard_map/ppermute | solution.py:1013
  95.7 0.8 copy-start
  171.4 61.5 %collective-permute-start.3 = (bf16[4,96,1792]{2,1,0:T(8,128)(2,1)}, bf16[4,96,1792]{2,1,0:T(8,128)(2,1)}, u32[]{:S(2)}, u32[]{:S(2)}) collective-permute-start(bf16[4,96,1792]{2,1,0:T(8,128)(2,1)} %get-tuple-element.67), channel_id=1, source_target_pairs={{0,4},{4,0},{8,12},{12,8},{16,20},{20,16},{24,28},{28,24},{1,5},{5... | collective-permute-start | bytes 4128776 | tf_op jit(solution)/shard_map/ppermute | solution.py:349
  172.0 60.9 %collective-permute-start.4 = (bf16[4,96,1792]{2,1,0:T(8,128)(2,1)}, bf16[4,96,1792]{2,1,0:T(8,128)(2,1)}, u32[]{:S(2)}, u32[]{:S(2)}) collective-permute-start(bf16[4,96,1792]{2,1,0:T(8,128)(2,1)} %get-tuple-element.68), channel_id=1, source_target_pairs={{0,2},{1,3},{2,0},{3,1},{4,6},{5,7},{6,4},{7,5},{8,10},{9,11},{10,... | collective-permute-start | bytes 4128776 | tf_op jit(solution)/shard_map/ppermute | solution.py:345
  172.4 60.5 %collective-permute-start.5 = (bf16[4,96,1792]{2,1,0:T(8,128)(2,1)}, bf16[4,96,1792]{2,1,0:T(8,128)(2,1)}, u32[]{:S(2)}, u32[]{:S(2)}) collective-permute-start(bf16[4,96,1792]{2,1,0:T(8,128)(2,1)} %get-tuple-element.69), channel_id=1, source_target_pairs={{0,6},{1,7},{2,4},{3,5},{4,2},{5,3},{6,0},{7,1},{8,14},{9,15},{10,... | collective-permute-start | bytes 4128776 | tf_op jit(solution)/shard_map/ppermute | solution.py:1013
where the time goes:
time: 291 us; the launch traced here: 285 us
  Pallas kernels  271 us (93%)
  starting transfers between devices  7.11 us (2%)
  waiting for transfers between devices  4.85 us (2%)
    pallas_call x1, Pallas kernels, middle(): pl.pallas_call(functools.partial(middle_kernel, with_w), out_shape=(sd((R...  74.9 us
    pallas_call x1, Pallas kernels, attn_bwd(): pl.pallas_call(functools.partial(bwd_kernel, heads), out_shape=(sd((n * H...  57.9 us
    pallas_call x1, Pallas kernels, final(): pl.pallas_call(functools.partial(final_kernel, with_w), out_shape=shapes,...  48.4 us
    pallas_call x1, Pallas kernels, gather_start(): pl.pallas_call(functools.partial(gather_kernel, with_w), out_shape=shapes...  46 us
    pallas_call x1, Pallas kernels, attn_fwd(): pl.pallas_call(fwd_kernel, out_shape=(sd((n, S), bf), sd((S, 2 * n), bf),...  40.6 us
  transfers between devices with their start and end apart: 6, of which 1 were waited for; matrix products, arithmetic and copies ran while one was open for 0% of the time, Pallas kernels for 35%

commit v1 on v0

--- a/solution.py
+++ b/solution.py
@@ -20,6 +20,8 @@
 BP = 4
 BTQ = 1024
 BTK = 256
+FQT = 1024
+FKT = 512
 VM = pl.BlockSpec(memory_space=pltpu.VMEM)
 SM = pl.BlockSpec(memory_space=pltpu.SMEM)
 HB = pl.BlockSpec(memory_space=pltpu.HBM)
@@ -107,46 +109,109 @@
         c.start()
     zero = jnp.zeros((HD, TQ), bf)
 
-    def tile(i, _):
-        qz = [jnp.concatenate([qt_ref[h * HD:(h + 1) * HD, aligned(i, TQ)], zero], 0) for h in range(HN)]
-        m, acc = [None] * HN, [None] * HN
-        for c in range(TRUNK // TK):
-            ks = slice(c * TK, (c + 1) * TK)
-            s = [mm(kv_ref[ks, h * 128:(h + 1) * 128], qz[h]) for h in range(HN)]
-            new = [jnp.max(x, axis=0, keepdims=True) for x in s]
-            if c:
-                new = [jnp.maximum(x, y) for x, y in zip(m, new)]
-            p = [jnp.exp(x - y).astype(bf) for x, y in zip(s, new)]
+    square = lambda ref, h, cols: jnp.sum(jnp.square(ref[h * HD:(h + 1) * HD, cols].astype(f32)), axis=0, keepdims=True)
+
+    def norms(i, best):
+        cols = aligned(i, BLK)
+        for h in range(HN):
+            m_s[i, h:h + 1] = square(qt_ref, h, cols)
+        return tuple(jnp.maximum(best[h], square(kt_ref, h, cols)) for h in range(HN))
+
+    best = lax.fori_loop(0, NB, norms, tuple(jnp.zeros((1, BLK), f32) for h in range(HN)))
+    most = [jnp.max(x, axis=1, keepdims=True) for x in best]
+
+    def bounds(i, _):
+        for h in range(HN):
+            m_s[i, h:h + 1] = jnp.sqrt(m_s[i, h:h + 1] * most[h]) * 1.001
+        return 0
+
+    lax.fori_loop(0, NB, bounds, 0)
+    m_s[NB] = jnp.zeros((8, BLK), f32)
+    wide_zero = jnp.zeros((HD, FQT), bf)
+
+    def fast_tile(i, _):
+        per = FQT // BLK
+        qz = [jnp.concatenate([qt_ref[h * HD:(h + 1) * HD, aligned(i, FQT)], wide_zero], 0) for h in range(HN)]
+        m = [jnp.concatenate([m_s[i * per + j, h:h + 1] for j in range(per)], 1) for h in range(HN)]
+        acc = [None] * HN
+        for c in range(TRUNK // FKT):
+            ks = slice(c * FKT, (c + 1) * FKT)
+            p = [jnp.exp(mm(kv_ref[ks, h * 128:(h + 1) * 128], qz[h]) - m[h]).astype(bf) for h in range(HN)]
             a = [mm(vt_ref[h, :, ks], p[h]) for h in range(HN)]
-            if c:
-                a = [x * jnp.exp(y - z) + w for x, y, z, w in zip(acc, m, new, a)]
-            m, acc = new, a
+            acc = [x + y for x, y in zip(acc, a)] if c else a
         for h in range(HN):
-            for j in range(TQ // BLK):
-                acc_s[i * (TQ // BLK) + j, h] = acc[h][:, j * BLK:(j + 1) * BLK]
-                m_s[i * (TQ // BLK) + j, h:h + 1] = m[h][:, j * BLK:(j + 1) * BLK]
+            for j in range(per):
+                acc_s[i * per + j, h] = acc[h][:, j * BLK:(j + 1) * BLK]
         return 0
 
-    lax.fori_loop(0, NB * BLK // TQ, tile, 0)
-
-    def step(g, _):
+    lax.fori_loop(0, NB * BLK // FQT, fast_tile, 0)
+
+    def pick(g):
         work = []
         for p in range(FP):
             q, kb = pairs[0, g * FP + p], jnp.minimum(pairs[1, g * FP + p], NB - 1)
             work += [(q, aligned(jnp.minimum(q, NB - 1), BLK), aligned(kb, BLK), h) for h in range(HN)]
-        s = [mm(kv_ref[ks, h * 128:(h + 1) * 128],
-                jnp.concatenate([qt_ref[h * HD:(h + 1) * HD, qs], zero[:, :BLK]], 0)) for q, qs, ks, h in work]
-        m = [m_s[q, h:h + 1] for q, qs, ks, h in work]
-        new = [jnp.maximum(y, jnp.max(x, axis=0, keepdims=True)) for x, y in zip(s, m)]
-        p = [jnp.exp(x - y).astype(bf) for x, y in zip(s, new)]
-        a = [mm(vt_ref[h, :, ks], x) for x, (q, qs, ks, h) in zip(p, work)]
-        a = [acc_s[q, h] * jnp.exp(x - y) + z for x, y, z, (q, qs, ks, h) in zip(m, new, a, work)]
-        for x, y, (q, qs, ks, h) in zip(new, a, work):
-            m_s[q, h:h + 1] = x
+        return work
+
+    def scores(work):
+        return [mm(kv_ref[ks, h * 128:(h + 1) * 128],
+                   jnp.concatenate([qt_ref[h * HD:(h + 1) * HD, qs], zero[:, :BLK]], 0)) for q, qs, ks, h in work]
+
+    def fast_step(g, _):
+        work = pick(g)
+        p = [jnp.exp(x - m_s[q, h:h + 1]).astype(bf) for x, (q, qs, ks, h) in zip(scores(work), work)]
+        a = [acc_s[q, h] + mm(vt_ref[h, :, ks], x) for x, (q, qs, ks, h) in zip(p, work)]
+        for y, (q, qs, ks, h) in zip(a, work):
             acc_s[q, h] = y
         return 0
 
-    lax.fori_loop(0, pairs[2, 0] // FP, step, 0)
+    lax.fori_loop(0, pairs[2, 0] // FP, fast_step, 0)
+
+    def small(i, bad):
+        for h in range(HN):
+            bad = jnp.where(acc_s[i, h, HD:HD + 1, :] > 1e-18, bad, 1.0)
+        return bad
+
+    bad = jnp.max(lax.fori_loop(0, NB, small, jnp.zeros((1, BLK), f32)))
+
+    @pl.when(bad > 0)
+    def _():
+        def tile(i, _):
+            qz = [jnp.concatenate([qt_ref[h * HD:(h + 1) * HD, aligned(i, TQ)], zero], 0) for h in range(HN)]
+            m, acc = [None] * HN, [None] * HN
+            for c in range(TRUNK // TK):
+                ks = slice(c * TK, (c + 1) * TK)
+                s = [mm(kv_ref[ks, h * 128:(h + 1) * 128], qz[h]) for h in range(HN)]
+                new = [jnp.max(x, axis=0, keepdims=True) for x in s]
+                if c:
+                    new = [jnp.maximum(x, y) for x, y in zip(m, new)]
+                p = [jnp.exp(x - y).astype(bf) for x, y in zip(s, new)]
+                a = [mm(vt_ref[h, :, ks], p[h]) for h in range(HN)]
+                if c:
+                    a = [x * jnp.exp(y - z) + w for x, y, z, w in zip(acc, m, new, a)]
+                m, acc = new, a
+            for h in range(HN):
+                for j in range(TQ // BLK):
+                    acc_s[i * (TQ // BLK) + j, h] = acc[h][:, j * BLK:(j + 1) * BLK]
+                    m_s[i * (TQ // BLK) + j, h:h + 1] = m[h][:, j * BLK:(j + 1) * BLK]
+            return 0
+
+        lax.fori_loop(0, NB * BLK // TQ, tile, 0)
+
+        def step(g, _):
+            work = pick(g)
+            s = scores(work)
+            m = [m_s[q, h:h + 1] for q, qs, ks, h in work]
+            new = [jnp.maximum(y, jnp.max(x, axis=0, keepdims=True)) for x, y in zip(s, m)]
+            p = [jnp.exp(x - y).astype(bf) for x, y in zip(s, new)]
+            a = [mm(vt_ref[h, :, ks], x) for x, (q, qs, ks, h) in zip(p, work)]
+            a = [acc_s[q, h] * jnp.exp(x - y) + z for x, y, z, (q, qs, ks, h) in zip(m, new, a, work)]
+            for x, y, (q, qs, ks, h) in zip(new, a, work):
+                m_s[q, h:h + 1] = x
+                acc_s[q, h] = y
+            return 0
+
+        lax.fori_loop(0, pairs[2, 0] // FP, step, 0)
 
     rank = lax.axis_index("tensor")
 
@@ -489,7 +554,7 @@
     keep(whole.at[rd], whole_hbm.at[rd])
     if with_w:
         keep(gz, gz_hbm)
-        keep(gz.at[pl.ds(0, 2)], gl_hbm)
+        keep(gz.at[pl.ds(0, 2), :, pl.ds(0, OU)], gl_hbm)
         side(0, z).wait()
         for s in (1, 2, 3):
             for way in (0, 1):
@@ -527,7 +592,7 @@
     if with_w:
         part = weights[0].shape[1]
         line = jax.ShapeDtypeStruct((4, part, PK), bf)
-        shapes += [jax.ShapeDtypeStruct((8, part, 3 * QW), bf), line, jax.ShapeDtypeStruct((2, part, PK), bf)]
+        shapes += [jax.ShapeDtypeStruct((8, part, 3 * QW), bf), line, jax.ShapeDtypeStruct((2, part, OU), bf)]
         scratch = [pltpu.VMEM((D, 8), f32)]
         sems += [dma((2, 6)), dma((2, 6)), dma((7,)), dma((7,))]
     return pl.pallas_call(
@@ -576,7 +641,9 @@
 
     def heads_in(b, m):
         cols = pl.ds(b * RB, RB)
-        return remote(mix.at[m, :, cols], mixr.at[m, :, cols], asend.at[b, m], arecv.at[b, m], devices[m])
+        k = lax.axis_index("tensor")
+        peer = {"tensor": (k, flip1(k), lax.rem(k + 2, 4), 3 - k)[m]}
+        return remote(mix.at[m, :, cols], mixr.at[m, :, cols], asend.at[b, m], arecv.at[b, m], peer)
 
     def heads_out(b, m):
         cols = aligned(b, RB)
@@ -594,12 +661,17 @@
         other = lax.rem(rank + 2, 4)
         four, two, end = pl.ds(0, 4), pl.ds(0, 2), pl.ds(2, 2)
         near = {"tensor": flip1(rank)}
-        relay(remote(wc.at[end, :, span], w.at[other, end, side, :, span], xsend.at[j], xrecv.at[j],
-                     {"dp": flip1(lax.axis_index("dp"))}))
+        if relay is not None:
+            relay(remote(wc.at[end, :, span], w.at[other, end, side, :, span], xsend.at[j], xrecv.at[j],
+                         {"dp": flip1(lax.axis_index("dp"))}))
+            if j:
+                relay(remote(wb.at[two, :, span], w.at[rank, two, 1 - side, :, span], xsend.at[2], xrecv.at[2],
+                             {"tensor": other}))
         pieces = ((wa, rank, four, side), (wb, rank, four, 1 - side), (wc, other, four, side), (wd, other, two, 1 - side))
-        for i, (ref, t, zz, at) in enumerate(pieces):
+        for i, (ref, t, zz, at) in enumerate(pieces[:4 - j]):
             src, dst = ref.at[:, :, span], w.at[t, zz, at, :, span]
-            hand(remote(src, dst, wsend.at[j, i], wrecv.at[j, i], near))
+            if hand is not None:
+                hand(remote(src, dst, wsend.at[j, i], wrecv.at[j, i], near))
             if place is not None:
                 place(pltpu.make_async_copy(src, dst, loc.at[11 + 4 * j + i]))
 
@@ -609,34 +681,32 @@
 
     def weight_tail(j):
         rank, side = lax.axis_index("tensor"), lax.rem(lax.axis_index("dp"), 2)
-        tail = w.at[lax.rem(rank + 2, 4), pl.ds(2, 2), 1 - side, :, (pl.ds(0, OU), pl.ds(OU, FQ))[j]]
+        tail = w.at[lax.rem(rank + 2, 4), (pl.ds(2, 2), pl.ds(0, 4))[j], 1 - side, :, (pl.ds(0, OU), pl.ds(OU, FQ))[j]]
         return remote(tail, tail, wsend.at[j, 4], wrecv.at[j, 4], {"tensor": flip1(rank)})
 
     if with_w:
-        for j in (0, 1):
-            weight_moves(j, lambda c: c.start(), lambda c: c.start(), lambda c: c.start())
+        weight_moves(0, lambda c: c.start(), lambda c: c.start(), lambda c: c.start())
     else:
         for j in (0, 1):
             whole_fill(j).start()
-    for part in heads[1:]:
-        for c in part:
-            c.start()
     sums_o[...] = jnp.zeros_like(sums_o)
     out_bias, outer_bias = (v[...].astype(f32).reshape(1, D) for v in (ob, fb))
     gains, shifts = ng[...].astype(f32), ns[...].astype(f32)
     gain1, gain2, shift1, shift2 = gains[0:1], gains[1:2], shifts[0:1], shifts[1:2]
     def weights_here(j):
         if with_w:
-            def arrived(c):
-                c.wait_recv()
-                weight_tail(j).start()
-
-            weight_moves(j, arrived, lambda c: c.wait_recv(), lambda c: c.wait())
+            weight_moves(j, lambda c: c.wait_recv(), None, None)
+            weight_tail(j).start()
+            weight_moves(j, None, lambda c: c.wait_recv(), lambda c: c.wait())
             weight_tail(j).wait_recv()
         else:
             whole_fill(j).wait()
 
     weights_here(0)
+    for c in heads[0]:
+        c.wait_recv()
+    if with_w:
+        weight_moves(1, lambda c: c.start(), lambda c: c.start(), lambda c: c.start())
     fill.wait()
     for c in rows_in:
         c.wait()
@@ -650,7 +720,7 @@
         sums_o[i:i + 1] += jnp.sum(rows, axis=0, keepdims=True)
 
     def block(b, _):
-        for i in range(NR):
+        for i in range(1, NR):
             @pl.when(b == i)
             def _():
                 for c in heads[i]:
@@ -672,6 +742,9 @@
         @pl.when(b == 0)
         def _():
             weights_here(1)
+            for i in range(1, NR):
+                for m in (3, 2, 1):
+                    heads_in(i, m).start()
 
         mlp = outer_bias
         for t in range(4):
@@ -779,7 +852,7 @@
     with_w = len(weights) > 1
     vm = pltpu.VMEM
     tokens = (D, ROWS)
-    extra = [vm((7, 16, D), f32), vm((4, 16, D), f32), dma((2,)), dma((2,)), dma((2, 5)), dma((2, 5)),
+    extra = [vm((7, 16, D), f32), vm((4, 16, D), f32), dma((3,)), dma((3,)), dma((2, 5)), dma((2, 5)),
              dma((6,)), dma((6,))] if with_w else []
     return pl.pallas_call(
         functools.partial(middle_kernel, with_w),

time: 291 us -> 316 us (1.086)
  Pallas kernels: 271 us -> 298 us
    pallas_call x1, Pallas kernels: 40.6 us -> 57.4 us  [attn_fwd(): pl.pallas_call(fwd_kernel, out_shape=(sd((n, S), bf), sd((S, 2 * n), bf),...]
    pallas_call x1, Pallas kernels: 74.9 us -> 91.3 us  [middle(): pl.pallas_call(functools.partial(middle_kernel, with_w), out_shape=(sd((R...]
    pallas_call x1, Pallas kernels: 57.9 us -> 54 us  [attn_bwd(): pl.pallas_call(functools.partial(bwd_kernel, heads), out_shape=(sd((n * H...]
  transfers between devices with their start and end apart: 6 -> 6, of which waited for: 1 -> 1; matrix products, arithmetic and copies ran while one was open for 0% -> 0% of each run, Pallas kernels for 35% -> 36%
where the time goes in v1:
time: 316 us; the launch traced here: 311 us
  Pallas kernels  298 us (94%)
  starting transfers between devices  7.11 us (2%)
  waiting for transfers between devices  4.52 us (1%)
    pallas_call x1, Pallas kernels, middle(): pl.pallas_call(functools.partial(middle_kernel, with_w), out_shape=(sd((R...  91.3 us
    pallas_call x1, Pallas kernels, attn_fwd(): pl.pallas_call(fwd_kernel, out_shape=(sd((n, S), bf), sd((S, 2 * n), bf),...  57.4 us
    pallas_call x1, Pallas kernels, attn_bwd(): pl.pallas_call(functools.partial(bwd_kernel, heads), out_shape=(sd((n * H...  54 us
    pallas_call x1, Pallas kernels, gather_start(): pl.pallas_call(functools.partial(gather_kernel, with_w), out_shape=shapes...  45.9 us
    pallas_call x1, Pallas kernels, final(): pl.pallas_call(functools.partial(final_kernel, with_w), out_shape=shapes,...  45.6 us
  transfers between devices with their start and end apart: 6, of which 1 were waited for; matrix products, arithmetic and copies ran while one was open for 0% of the time, Pallas kernels for 36%

profile of v1, /device:TPU:0, one launch (start us, length us, event | category | flops | bytes accessed | tf_op | source)
XLA Modules:
  0.0 311.0 jit_solution(8280506762424067311)
XLA Ops:
  0.6 45.9 %gather_start.1 = (bf16[4,1024,768]{2,1,0:T(8,128)(2,1)}, bf16[8,96,576]{2,1,0:T(8,128)(2,1)}, bf16[4,96,1792]{2,1,0:T(8,128)(2,1)}, bf16[2,96,1024]{2,1,0:T(8,128)(2,1)}) custom-call(bf16[1024,768]{1,0:T(8,128)(2,1)} %refs_5_.3, bf16[1,768]{1,0:T(2,128)(2,1)} %refs_6_.3, bf16[3,96,192]{2,1,0:T(8,128)(2,1)} %bitcast.4, bf16[96,768]{1,0:T(8,128)(2,1)} %refs_3_.1, ...), custom_call_target="tpu_custom_call" | custom-call | tf_op jit(solution)/shard_map/gather_start/pallas_call | solution.py:598
  46.5 0.5 collective-permute-start.1
  47.0 1.5 collective-permute-start
  48.5 1.5 collective-permute-start.2
  50.1 57.4 %tree_attention.1 = (bf16[192,4096]{1,0:T(8,128)(2,1)}, bf16[4096,384]{1,0:T(8,128)(2,1)}, bf16[192,4096]{1,0:T(8,128)(2,1)}, f32[192,4096]{1,0:T(8,128)}, bf16[...) custom-call(s32[1,13]{1,0:T(1,128)} %parents.1, ...), custom_call_target="tpu_custom_call" | custom-call | flops 40000000000 | bytes 12000000 | tf_op jit(solution)/shard_map/tree_attention/pallas_call | solution.py:243
  107.5 0.0 collective-permute-done.2.refs_3_
  107.5 0.0 copy-start
  107.5 0.0 collective-permute-done.1.refs_2_
  107.5 0.0 collective-permute-done.refs_1_
  107.5 0.7 copy-done
  108.2 91.3 %middle.1 = (bf16[1024,768]{1,0:T(8,128)(2,1)}, f32[1024,768]{1,0:T(8,128)}, bf16[4,192,1024]{2,1,0:T(8,128)(2,1)}, bf16[4,96,1792]{2,1,0:T(8,128)(2,1)}, bf16[4...) custom-call(bf16[4,96,1792]{2,1,0:T(8,128)(2,1)} %get-tuple-element.55., ...), custom_call_target="tpu_custom_call" | custom-call | flops 32999999488 | bytes 50000000 | tf_op jit(solution)/shard_map/middle/pallas_call | solution.py:857
  199.5 0.7 collective-permute-start.3
  200.3 0.9 collective-permute-start.4
  201.2 1.9 collective-permute-start.5
  203.1 54.0 %tree_attention_grad.1 = (bf16[192,4096]{1,0:T(8,128)(2,1)}, bf16[4096,384]{1,0:T(8,128)(2,1)}, bf16[1024,768]{1,0:T(8,128)(2,1)}) custom-call(s32[3,192]{1,0:T(4,128)} %get-tuple-element.51.pairs, bf16[192,4096]{1,0:T(8,128)(2,1)} %get-tuple-element.52.qt_hbm, bf16[4096,384]{1,0:T(8,128)(2,1)} %get-tuple-element.53.kv_hbm, ...), custom_call_target="tpu_custom_call" | custom-call | flops 60000002048 | bytes 24000000 | tf_op jit(solution)/shard_map/tree_attention_grad/pallas_call | solution.py:357
  257.1 0.0 collective-permute-done.3.refs_6_
  257.1 0.0 collective-permute-done.4.refs_7_
  257.1 4.5 %collective-permute-done.5.refs_8_ = bf16[4,96,1792]{2,1,0:T(8,128)(2,1)} collective-permute-done((bf16[4,96,1792]{2,1,0:T(8,128)(2,1)}, bf16[4,96,1792]{2,1,0:T(8,128)(2,1)}, u32[]{:S(2)}, u32[]{:S(2)}) %collective-permute-start.5) | collective-permute-done | bytes 1376288 | tf_op jit(solution)/shard_map/ppermute | solution.py:1086
  261.6 45.6 %final.1 = (bf16[1024,768]{1,0:T(8,128)(2,1)}, f32[8,192]{1,0:T(8,128)}, f32[96,576]{1,0:T(8,128)}, f32[96,1792]{1,0:T(8,128)}) custom-call(bf16[4,1024,768]{2,1,0:T(8,128)(2,1)} %get-tuple-element.49.x_hbm.refs_0_, bf16[8,96,576]{2,1,0:T(8,128)(2,1)} %get-tuple-element.50.w_hbm.refs_1_, bf16[192,4096]{1,0:T(8,128)(2,1)} %get-tuple-element.63.refs_2_, ...), custom_call_target="tpu_custom_call" | custom-call | tf_op jit(solution)/shard_map/final/pallas_call | solution.py:1016
  307.2 3.6 %emit.1 = (bf16[1024,768]{1,0:T(8,128)(2,1)}, f32[3,96,192]{2,1,0:T(8,128)}, f32[2,192]{1,0:T(2,128)}, f32[192,96]{1,0:T(8,128)}, f32[768]{0:T(1024)}, /*index=5...) custom-call(bf16[1024,768]{1,0:T(8,128)(2,1)} %get-tuple-element.70., ...), custom_call_target="tpu_custom_call" | custom-call | tf_op jit(solution)/shard_map/emit/pallas_call | solution.py:1060
Async XLA Ops:
  46.5 61.0 %collective-permute-start.1 = (bf16[4,96,1792]{2,1,0:T(8,128)(2,1)}, bf16[4,96,1792]{2,1,0:T(8,128)(2,1)}, u32[]{:S(2)}, u32[]{:S(2)}) collective-permute-start(bf16[4,96,1792]{2,1,0:T(8,128)(2,1)} %get-tuple-element.55.refs_0_), channel_id=1, source_target_pairs={{0,2},{1,3},{2,0},{3,1},{4,6},{5,7},{6,4},{7,5},{8,10},{9,11},{10,... | collective-permute-start | bytes 4128776 | tf_op jit(solution)/shard_map/ppermute | solution.py:410
  47.0 60.5 %collective-permute-start = (bf16[4,96,1792]{2,1,0:T(8,128)(2,1)}, bf16[4,96,1792]{2,1,0:T(8,128)(2,1)}, u32[]{:S(2)}, u32[]{:S(2)}) collective-permute-start(bf16[4,96,1792]{2,1,0:T(8,128)(2,1)} %get-tuple-element.55.refs_0_), channel_id=1, source_target_pairs={{0,4},{4,0},{8,12},{12,8},{16,20},{20,16},{24,28},{28,24},{1,5},{5... | collective-permute-start | bytes 4128776 | tf_op jit(solution)/shard_map/ppermute | solution.py:414
  48.5 58.9 %collective-permute-start.2 = (bf16[2,96,1024]{2,1,0:T(8,128)(2,1)}, bf16[2,96,1024]{2,1,0:T(8,128)(2,1)S(1)}, u32[]{:S(2)}, u32[]{:S(2)}) collective-permute-start(bf16[2,96,1024]{2,1,0:T(8,128)(2,1)} %get-tuple-element.56), channel_id=1, source_target_pairs={{0,6},{1,7},{2,4},{3,5},{4,2},{5,3},{6,0},{7,1},{8,14},{9,15},{10,... | collective-permute-start | bytes 1179656 | tf_op jit(solution)/shard_map/ppermute | solution.py:1086
  107.5 0.8 copy-start
  199.5 57.6 %collective-permute-start.3 = (bf16[4,96,1792]{2,1,0:T(8,128)(2,1)}, bf16[4,96,1792]{2,1,0:T(8,128)(2,1)}, u32[]{:S(2)}, u32[]{:S(2)}) collective-permute-start(bf16[4,96,1792]{2,1,0:T(8,128)(2,1)} %get-tuple-element.67), channel_id=1, source_target_pairs={{0,4},{4,0},{8,12},{12,8},{16,20},{20,16},{24,28},{28,24},{1,5},{5... | collective-permute-start | bytes 4128776 | tf_op jit(solution)/shard_map/ppermute | solution.py:414
  200.3 56.8 %collective-permute-start.4 = (bf16[4,96,1792]{2,1,0:T(8,128)(2,1)}, bf16[4,96,1792]{2,1,0:T(8,128)(2,1)}, u32[]{:S(2)}, u32[]{:S(2)}) collective-permute-start(bf16[4,96,1792]{2,1,0:T(8,128)(2,1)} %get-tuple-element.68), channel_id=1, source_target_pairs={{0,2},{1,3},{2,0},{3,1},{4,6},{5,7},{6,4},{7,5},{8,10},{9,11},{10,... | collective-permute-start | bytes 4128776 | tf_op jit(solution)/shard_map/ppermute | solution.py:410
  201.2 60.4 %collective-permute-start.5 = (bf16[4,96,1792]{2,1,0:T(8,128)(2,1)}, bf16[4,96,1792]{2,1,0:T(8,128)(2,1)}, u32[]{:S(2)}, u32[]{:S(2)}) collective-permute-start(bf16[4,96,1792]{2,1,0:T(8,128)(2,1)} %get-tuple-element.69), channel_id=1, source_target_pairs={{0,6},{1,7},{2,4},{3,5},{4,2},{5,3},{6,0},{7,1},{8,14},{9,15},{10,... | collective-permute-start | bytes 4128776 | tf_op jit(solution)/shard_map/ppermute | solution.py:1086

commit v2 on v1

--- a/solution.py
+++ b/solution.py
@@ -47,12 +47,13 @@
             pairs[1, n] = c + 3
             cur[s] = jnp.where(c > 0, parents[0, c], 0)
             n = n + jnp.where(c > 0, 1, 0)
-        for i in range(PAD - 1):
-            pairs[0, n + i] = jnp.int32(NB)
-            pairs[1, n + i] = jnp.int32(NB)
-        return (n + PAD - 1) // PAD * PAD
-
-    pairs[2, 0] = lax.fori_loop(0, SEGS - 1, level, jnp.int32(0))
+        return n
+
+    n = lax.fori_loop(0, SEGS - 1, level, jnp.int32(0))
+    for i in range(PAD - 1):
+        pairs[0, n + i] = jnp.int32(NB)
+        pairs[1, n + i] = jnp.int32(NB)
+    pairs[2, 0] = (n + PAD - 1) // PAD * PAD
 
 
 PR = 1024
@@ -146,10 +147,10 @@
 
     lax.fori_loop(0, NB * BLK // FQT, fast_tile, 0)
 
-    def pick(g):
+    def pick(g, count):
         work = []
-        for p in range(FP):
-            q, kb = pairs[0, g * FP + p], jnp.minimum(pairs[1, g * FP + p], NB - 1)
+        for p in range(count):
+            q, kb = pairs[0, g * count + p], jnp.minimum(pairs[1, g * count + p], NB - 1)
             work += [(q, aligned(jnp.minimum(q, NB - 1), BLK), aligned(kb, BLK), h) for h in range(HN)]
         return work
 
@@ -158,11 +159,11 @@
                    jnp.concatenate([qt_ref[h * HD:(h + 1) * HD, qs], zero[:, :BLK]], 0)) for q, qs, ks, h in work]
 
     def fast_step(g, _):
-        work = pick(g)
+        work = pick(g, FP)
         p = [jnp.exp(x - m_s[q, h:h + 1]).astype(bf) for x, (q, qs, ks, h) in zip(scores(work), work)]
-        a = [acc_s[q, h] + mm(vt_ref[h, :, ks], x) for x, (q, qs, ks, h) in zip(p, work)]
+        a = [mm(vt_ref[h, :, ks], x) for x, (q, qs, ks, h) in zip(p, work)]
         for y, (q, qs, ks, h) in zip(a, work):
-            acc_s[q, h] = y
+            acc_s[q, h] += y
         return 0
 
     lax.fori_loop(0, pairs[2, 0] // FP, fast_step, 0)
@@ -199,7 +200,7 @@
         lax.fori_loop(0, NB * BLK // TQ, tile, 0)
 
         def step(g, _):
-            work = pick(g)
+            work = pick(g, 1)
             s = scores(work)
             m = [m_s[q, h:h + 1] for q, qs, ks, h in work]
             new = [jnp.maximum(y, jnp.max(x, axis=0, keepdims=True)) for x, y in zip(s, m)]
@@ -211,7 +212,7 @@
                 acc_s[q, h] = y
             return 0
 
-        lax.fori_loop(0, pairs[2, 0] // FP, step, 0)
+        lax.fori_loop(0, pairs[2, 0], step, 0)
 
     rank = lax.axis_index("tensor")
 

time: 316 us -> 318 us (level)
    ppermute x2, waiting for transfers between devices: 0.01 us -> 5 us  [partner(): return lax.ppermute(x, 'tensor', [(i, i ^ mask) for i in range(4)])]
    pallas_call x1, Pallas kernels: 57.4 us -> 62.2 us  [attn_fwd(): pl.pallas_call(fwd_kernel, out_shape=(sd((n, S), bf), sd((S, 2 * n), bf),...]
    ppermute x2, waiting for transfers between devices: 4.51 us -> 0.01 us  [on_device(): cross = lambda a: lax.ppermute(a, ('dp', 'tensor'), diagonal)]
    pallas_call x1, Pallas kernels: 91.3 us -> 87.6 us  [middle(): pl.pallas_call(functools.partial(middle_kernel, with_w), out_shape=(sd((R...]
  transfers between devices with their start and end apart: 6 -> 6, of which waited for: 1 -> 1; matrix products, arithmetic and copies ran while one was open for 0% -> 0% of each run, Pallas kernels for 36% -> 37%
where the time goes in v2:
time: 318 us; the launch traced here: 313 us
  Pallas kernels  299 us (94%)
  starting transfers between devices  7.11 us (2%)
  waiting for transfers between devices  5.01 us (2%)
    pallas_call x1, Pallas kernels, middle(): pl.pallas_call(functools.partial(middle_kernel, with_w), out_shape=(sd((R...  87.6 us
    pallas_call x1, Pallas kernels, attn_fwd(): pl.pallas_call(fwd_kernel, out_shape=(sd((n, S), bf), sd((S, 2 * n), bf),...  62.2 us
    pallas_call x1, Pallas kernels, attn_bwd(): pl.pallas_call(functools.partial(bwd_kernel, heads), out_shape=(sd((n * H...  53.8 us
    pallas_call x1, Pallas kernels, gather_start(): pl.pallas_call(functools.partial(gather_kernel, with_w), out_shape=shapes...  45.9 us
    pallas_call x1, Pallas kernels, final(): pl.pallas_call(functools.partial(final_kernel, with_w), out_shape=shapes,...  45.6 us
  transfers between devices with their start and end apart: 6, of which 1 were waited for; matrix products, arithmetic and copies ran while one was open for 0% of the time, Pallas kernels for 37%

profile of v2, /device:TPU:0, one launch (start us, length us, event | category | flops | bytes accessed | tf_op | source)
XLA Modules:
  0.0 312.8 jit_solution(3705533817637008601)
XLA Ops:
  0.6 45.9 %gather_start.1 = (bf16[4,1024,768]{2,1,0:T(8,128)(2,1)}, bf16[8,96,576]{2,1,0:T(8,128)(2,1)}, bf16[4,96,1792]{2,1,0:T(8,128)(2,1)}, bf16[2,96,1024]{2,1,0:T(8,128)(2,1)}) custom-call(bf16[1024,768]{1,0:T(8,128)(2,1)} %refs_5_.3, bf16[1,768]{1,0:T(2,128)(2,1)} %refs_6_.3, bf16[3,96,192]{2,1,0:T(8,128)(2,1)} %bitcast.4, bf16[96,768]{1,0:T(8,128)(2,1)} %refs_3_.1, ...), custom_call_target="tpu_custom_call" | custom-call | tf_op jit(solution)/shard_map/gather_start/pallas_call | solution.py:599
  46.5 0.5 collective-permute-start.1
  47.0 1.5 collective-permute-start
  48.5 1.5 collective-permute-start.2
  50.1 62.2 %tree_attention.1 = (bf16[192,4096]{1,0:T(8,128)(2,1)}, bf16[4096,384]{1,0:T(8,128)(2,1)}, bf16[192,4096]{1,0:T(8,128)(2,1)}, f32[192,4096]{1,0:T(8,128)}, bf16[...) custom-call(s32[1,13]{1,0:T(1,128)} %parents.1, ...), custom_call_target="tpu_custom_call" | custom-call | flops 40000000000 | bytes 12000000 | tf_op jit(solution)/shard_map/tree_attention/pallas_call | solution.py:244
  112.3 0.0 collective-permute-done.2.refs_3_
  112.3 0.0 copy-start
  112.3 0.0 collective-permute-done.1.refs_2_
  112.4 0.0 collective-permute-done.refs_1_
  112.4 0.7 copy-done
  113.1 87.6 %middle.1 = (bf16[1024,768]{1,0:T(8,128)(2,1)}, f32[1024,768]{1,0:T(8,128)}, bf16[4,192,1024]{2,1,0:T(8,128)(2,1)}, bf16[4,96,1792]{2,1,0:T(8,128)(2,1)}, bf16[4...) custom-call(bf16[4,96,1792]{2,1,0:T(8,128)(2,1)} %get-tuple-element.55., ...), custom_call_target="tpu_custom_call" | custom-call | flops 32999999488 | bytes 50000000 | tf_op jit(solution)/shard_map/middle/pallas_call | solution.py:858
  200.7 0.9 collective-permute-start.3
  201.7 1.1 collective-permute-start.4
  202.8 1.5 collective-permute-start.5
  204.3 53.8 %tree_attention_grad.1 = (bf16[192,4096]{1,0:T(8,128)(2,1)}, bf16[4096,384]{1,0:T(8,128)(2,1)}, bf16[1024,768]{1,0:T(8,128)(2,1)}) custom-call(s32[3,192]{1,0:T(4,128)} %get-tuple-element.51.pairs, bf16[192,4096]{1,0:T(8,128)(2,1)} %get-tuple-element.52.qt_hbm, bf16[4096,384]{1,0:T(8,128)(2,1)} %get-tuple-element.53.kv_hbm, ...), custom_call_target="tpu_custom_call" | custom-call | flops 60000002048 | bytes 24000000 | tf_op jit(solution)/shard_map/tree_attention_grad/pallas_call | solution.py:358
  258.1 0.0 collective-permute-done.3.refs_6_
  258.1 5.0 %collective-permute-done.4.refs_7_ = bf16[4,96,1792]{2,1,0:T(8,128)(2,1)} collective-permute-done((bf16[4,96,1792]{2,1,0:T(8,128)(2,1)}, bf16[4,96,1792]{2,1,0:T(8,128)(2,1)}, u32[]{:S(2)}, u32[]{:S(2)}) %collective-permute-start.4) | collective-permute-done | bytes 1376288 | tf_op jit(solution)/shard_map/ppermute | solution.py:411
  263.1 0.0 collective-permute-done.5.refs_8_
  263.1 45.6 %final.1 = (bf16[1024,768]{1,0:T(8,128)(2,1)}, f32[8,192]{1,0:T(8,128)}, f32[96,576]{1,0:T(8,128)}, f32[96,1792]{1,0:T(8,128)}) custom-call(bf16[4,1024,768]{2,1,0:T(8,128)(2,1)} %get-tuple-element.49.x_hbm.refs_0_, bf16[8,96,576]{2,1,0:T(8,128)(2,1)} %get-tuple-element.50.w_hbm.refs_1_, bf16[192,4096]{1,0:T(8,128)(2,1)} %get-tuple-element.63.refs_2_, ...), custom_call_target="tpu_custom_call" | custom-call | tf_op jit(solution)/shard_map/final/pallas_call | solution.py:1017
  308.7 3.6 %emit.1 = (bf16[1024,768]{1,0:T(8,128)(2,1)}, f32[3,96,192]{2,1,0:T(8,128)}, f32[2,192]{1,0:T(2,128)}, f32[192,96]{1,0:T(8,128)}, f32[768]{0:T(1024)}, /*index=5...) custom-call(bf16[1024,768]{1,0:T(8,128)(2,1)} %get-tuple-element.70., ...), custom_call_target="tpu_custom_call" | custom-call | tf_op jit(solution)/shard_map/emit/pallas_call | solution.py:1061
Async XLA Ops:
  46.5 65.8 %collective-permute-start.1 = (bf16[4,96,1792]{2,1,0:T(8,128)(2,1)}, bf16[4,96,1792]{2,1,0:T(8,128)(2,1)}, u32[]{:S(2)}, u32[]{:S(2)}) collective-permute-start(bf16[4,96,1792]{2,1,0:T(8,128)(2,1)} %get-tuple-element.55.refs_0_), channel_id=1, source_target_pairs={{0,2},{1,3},{2,0},{3,1},{4,6},{5,7},{6,4},{7,5},{8,10},{9,11},{10,... | collective-permute-start | bytes 4128776 | tf_op jit(solution)/shard_map/ppermute | solution.py:411
  47.0 65.3 %collective-permute-start = (bf16[4,96,1792]{2,1,0:T(8,128)(2,1)}, bf16[4,96,1792]{2,1,0:T(8,128)(2,1)}, u32[]{:S(2)}, u32[]{:S(2)}) collective-permute-start(bf16[4,96,1792]{2,1,0:T(8,128)(2,1)} %get-tuple-element.55.refs_0_), channel_id=1, source_target_pairs={{0,4},{4,0},{8,12},{12,8},{16,20},{20,16},{24,28},{28,24},{1,5},{5... | collective-permute-start | bytes 4128776 | tf_op jit(solution)/shard_map/ppermute | solution.py:415
  48.5 63.8 %collective-permute-start.2 = (bf16[2,96,1024]{2,1,0:T(8,128)(2,1)}, bf16[2,96,1024]{2,1,0:T(8,128)(2,1)S(1)}, u32[]{:S(2)}, u32[]{:S(2)}) collective-permute-start(bf16[2,96,1024]{2,1,0:T(8,128)(2,1)} %get-tuple-element.56), channel_id=1, source_target_pairs={{0,6},{1,7},{2,4},{3,5},{4,2},{5,3},{6,0},{7,1},{8,14},{9,15},{10,... | collective-permute-start | bytes 1179656 | tf_op jit(solution)/shard_map/ppermute | solution.py:1087
  112.3 0.8 copy-start
  200.7 57.4 %collective-permute-start.3 = (bf16[4,96,1792]{2,1,0:T(8,128)(2,1)}, bf16[4,96,1792]{2,1,0:T(8,128)(2,1)}, u32[]{:S(2)}, u32[]{:S(2)}) collective-permute-start(bf16[4,96,1792]{2,1,0:T(8,128)(2,1)} %get-tuple-element.67), channel_id=1, source_target_pairs={{0,4},{4,0},{8,12},{12,8},{16,20},{20,16},{24,28},{28,24},{1,5},{5... | collective-permute-start | bytes 4128776 | tf_op jit(solution)/shard_map/ppermute | solution.py:415
  201.7 61.4 %collective-permute-start.4 = (bf16[4,96,1792]{2,1,0:T(8,128)(2,1)}, bf16[4,96,1792]{2,1,0:T(8,128)(2,1)}, u32[]{:S(2)}, u32[]{:S(2)}) collective-permute-start(bf16[4,96,1792]{2,1,0:T(8,128)(2,1)} %get-tuple-element.68), channel_id=1, source_target_pairs={{0,2},{1,3},{2,0},{3,1},{4,6},{5,7},{6,4},{7,5},{8,10},{9,11},{10,... | collective-permute-start | bytes 4128776 | tf_op jit(solution)/shard_map/ppermute | solution.py:411
  202.8 60.3 %collective-permute-start.5 = (bf16[4,96,1792]{2,1,0:T(8,128)(2,1)}, bf16[4,96,1792]{2,1,0:T(8,128)(2,1)}, u32[]{:S(2)}, u32[]{:S(2)}) collective-permute-start(bf16[4,96,1792]{2,1,0:T(8,128)(2,1)} %get-tuple-element.69), channel_id=1, source_target_pairs={{0,6},{1,7},{2,4},{3,5},{4,2},{5,3},{6,0},{7,1},{8,14},{9,15},{10,... | collective-permute-start | bytes 4128776 | tf_op jit(solution)/shard_map/ppermute | solution.py:1087

commit v3 on v2

--- a/solution.py
+++ b/solution.py
@@ -421,6 +421,8 @@
 
 CH = 4
 CROWS = ROWS // CH
+GH = 8
+GROWS = ROWS // GH
 
 
 def remote(src, dst, s, q, dev):
@@ -503,12 +505,12 @@
 
         own(0)
         side(0, z).start()
-    rows = [pl.ds(i * CROWS, CROWS) for i in range(CH)]
+    rows = [pl.ds(i * GROWS, GROWS) for i in range(GH)]
     yc = []
-    for i in range(CH):
+    for i in range(GH):
         mine = whole.at[r, rows[i]]
         yc.append(sends.go(mine, mine, ysend.at[i], yrecv.at[i], yy))
-    c0 = sends.go(whole.at[r], whole.at[r], csend.at[CH], crecv.at[CH], core)
+    c0 = sends.go(whole.at[r], whole.at[r], csend.at[GH], crecv.at[GH], core)
     if with_w:
         part = wqg.shape[1]
         gz[z, :, 0:FQ] = w1[...]
@@ -542,7 +544,7 @@
 
     keep(whole.at[r], whole_hbm.at[r])
     cc = []
-    for i in range(CH):
+    for i in range(GH):
         yc[i].wait_recv()
         part = whole.at[ry, rows[i]]
         cc.append(sends.go(part, part, csend.at[i], crecv.at[i], core))
@@ -589,7 +591,7 @@
     shapes = [jax.ShapeDtypeStruct((4, ROWS, D), bf)]
     args = [inp, te, *weights]
     scratch = []
-    sems = [dma((CH,)), dma((CH,)), dma((CH + 1,)), dma((CH + 1,)), dma((8,))]
+    sems = [dma((GH,)), dma((GH,)), dma((GH + 1,)), dma((GH + 1,)), dma((8,))]
     if with_w:
         part = weights[0].shape[1]
         line = jax.ShapeDtypeStruct((4, part, PK), bf)

time: 318 us -> 315 us (level)
  Pallas kernels: 299 us -> 294 us
  transfers between devices with their start and end apart: 6 -> 6, of which waited for: 1 -> 1; matrix products, arithmetic and copies ran while one was open for 0% -> 0% of each run, Pallas kernels for 37% -> 36%
where the time goes in v3:
time: 315 us; the launch traced here: 310 us
  Pallas kernels  294 us (93%)
  waiting for transfers between devices  7.2 us (2%)
  starting transfers between devices  7.11 us (2%)
    pallas_call x1, Pallas kernels, middle(): pl.pallas_call(functools.partial(middle_kernel, with_w), out_shape=(sd((R...  87.8 us
    pallas_call x1, Pallas kernels, attn_fwd(): pl.pallas_call(fwd_kernel, out_shape=(sd((n, S), bf), sd((S, 2 * n), bf),...  59.5 us
    pallas_call x1, Pallas kernels, attn_bwd(): pl.pallas_call(functools.partial(bwd_kernel, heads), out_shape=(sd((n * H...  51.9 us
    pallas_call x1, Pallas kernels, gather_start(): pl.pallas_call(functools.partial(gather_kernel, with_w), out_shape=shapes...  46 us
    pallas_call x1, Pallas kernels, final(): pl.pallas_call(functools.partial(final_kernel, with_w), out_shape=shapes,...  45.6 us
    ppermute x2, waiting for transfers between devices, partner(): return lax.ppermute(x, 'tensor', [(i, i ^ mask) for i in range(4)])  7.19 us
  transfers between devices with their start and end apart: 6, of which 1 were waited for; matrix products, arithmetic and copies ran while one was open for 0% of the time, Pallas kernels for 36%

profile of v3, /device:TPU:0, one launch (start us, length us, event | category | flops | bytes accessed | tf_op | source)
XLA Modules:
  0.0 310.4 jit_solution(14960280527448472615)
XLA Ops:
  0.6 46.0 %gather_start.1 = (bf16[4,1024,768]{2,1,0:T(8,128)(2,1)}, bf16[8,96,576]{2,1,0:T(8,128)(2,1)}, bf16[4,96,1792]{2,1,0:T(8,128)(2,1)}, bf16[2,96,1024]{2,1,0:T(8,128)(2,1)}) custom-call(bf16[1024,768]{1,0:T(8,128)(2,1)} %refs_5_.3, bf16[1,768]{1,0:T(2,128)(2,1)} %refs_6_.3, bf16[3,96,192]{2,1,0:T(8,128)(2,1)} %bitcast.4, bf16[96,768]{1,0:T(8,128)(2,1)} %refs_3_.1, ...), custom_call_target="tpu_custom_call" | custom-call | tf_op jit(solution)/shard_map/gather_start/pallas_call | solution.py:601
  46.7 0.5 collective-permute-start.1
  47.2 1.5 collective-permute-start
  48.7 1.5 collective-permute-start.2
  50.2 59.5 %tree_attention.1 = (bf16[192,4096]{1,0:T(8,128)(2,1)}, bf16[4096,384]{1,0:T(8,128)(2,1)}, bf16[192,4096]{1,0:T(8,128)(2,1)}, f32[192,4096]{1,0:T(8,128)}, bf16[...) custom-call(s32[1,13]{1,0:T(1,128)} %parents.1, ...), custom_call_target="tpu_custom_call" | custom-call | flops 40000000000 | bytes 12000000 | tf_op jit(solution)/shard_map/tree_attention/pallas_call | solution.py:244
  109.7 0.0 collective-permute-done.2.refs_3_
  109.7 0.0 copy-start
  109.7 0.0 collective-permute-done.1.refs_2_
  109.7 0.0 collective-permute-done.refs_1_
  109.7 0.7 copy-done
  110.5 87.8 %middle.1 = (bf16[1024,768]{1,0:T(8,128)(2,1)}, f32[1024,768]{1,0:T(8,128)}, bf16[4,192,1024]{2,1,0:T(8,128)(2,1)}, bf16[4,96,1792]{2,1,0:T(8,128)(2,1)}, bf16[4...) custom-call(bf16[4,96,1792]{2,1,0:T(8,128)(2,1)} %get-tuple-element.55., ...), custom_call_target="tpu_custom_call" | custom-call | flops 32999999488 | bytes 50000000 | tf_op jit(solution)/shard_map/middle/pallas_call | solution.py:860
  198.3 1.3 collective-permute-start.3
  199.6 0.8 collective-permute-start.4
  200.3 1.5 collective-permute-start.5
  201.8 51.9 %tree_attention_grad.1 = (bf16[192,4096]{1,0:T(8,128)(2,1)}, bf16[4096,384]{1,0:T(8,128)(2,1)}, bf16[1024,768]{1,0:T(8,128)(2,1)}) custom-call(s32[3,192]{1,0:T(4,128)} %get-tuple-element.51.pairs, bf16[192,4096]{1,0:T(8,128)(2,1)} %get-tuple-element.52.qt_hbm, bf16[4096,384]{1,0:T(8,128)(2,1)} %get-tuple-element.53.kv_hbm, ...), custom_call_target="tpu_custom_call" | custom-call | flops 60000002048 | bytes 24000000 | tf_op jit(solution)/shard_map/tree_attention_grad/pallas_call | solution.py:358
  253.8 0.0 collective-permute-done.3.refs_6_
  253.8 7.2 %collective-permute-done.4.refs_7_ = bf16[4,96,1792]{2,1,0:T(8,128)(2,1)} collective-permute-done((bf16[4,96,1792]{2,1,0:T(8,128)(2,1)}, bf16[4,96,1792]{2,1,0:T(8,128)(2,1)}, u32[]{:S(2)}, u32[]{:S(2)}) %collective-permute-start.4) | collective-permute-done | bytes 1376288 | tf_op jit(solution)/shard_map/ppermute | solution.py:411
  261.0 0.0 collective-permute-done.5.refs_8_
  261.0 45.6 %final.1 = (bf16[1024,768]{1,0:T(8,128)(2,1)}, f32[8,192]{1,0:T(8,128)}, f32[96,576]{1,0:T(8,128)}, f32[96,1792]{1,0:T(8,128)}) custom-call(bf16[4,1024,768]{2,1,0:T(8,128)(2,1)} %get-tuple-element.49.x_hbm.refs_0_, bf16[8,96,576]{2,1,0:T(8,128)(2,1)} %get-tuple-element.50.w_hbm.refs_1_, bf16[192,4096]{1,0:T(8,128)(2,1)} %get-tuple-element.63.refs_2_, ...), custom_call_target="tpu_custom_call" | custom-call | tf_op jit(solution)/shard_map/final/pallas_call | solution.py:1019
  306.6 3.6 %emit.1 = (bf16[1024,768]{1,0:T(8,128)(2,1)}, f32[3,96,192]{2,1,0:T(8,128)}, f32[2,192]{1,0:T(2,128)}, f32[192,96]{1,0:T(8,128)}, f32[768]{0:T(1024)}, /*index=5...) custom-call(bf16[1024,768]{1,0:T(8,128)(2,1)} %get-tuple-element.70., ...), custom_call_target="tpu_custom_call" | custom-call | tf_op jit(solution)/shard_map/emit/pallas_call | solution.py:1063
Async XLA Ops:
  46.7 63.0 %collective-permute-start.1 = (bf16[4,96,1792]{2,1,0:T(8,128)(2,1)}, bf16[4,96,1792]{2,1,0:T(8,128)(2,1)}, u32[]{:S(2)}, u32[]{:S(2)}) collective-permute-start(bf16[4,96,1792]{2,1,0:T(8,128)(2,1)} %get-tuple-element.55.refs_0_), channel_id=1, source_target_pairs={{0,2},{1,3},{2,0},{3,1},{4,6},{5,7},{6,4},{7,5},{8,10},{9,11},{10,... | collective-permute-start | bytes 4128776 | tf_op jit(solution)/shard_map/ppermute | solution.py:411
  47.2 62.5 %collective-permute-start = (bf16[4,96,1792]{2,1,0:T(8,128)(2,1)}, bf16[4,96,1792]{2,1,0:T(8,128)(2,1)}, u32[]{:S(2)}, u32[]{:S(2)}) collective-permute-start(bf16[4,96,1792]{2,1,0:T(8,128)(2,1)} %get-tuple-element.55.refs_0_), channel_id=1, source_target_pairs={{0,4},{4,0},{8,12},{12,8},{16,20},{20,16},{24,28},{28,24},{1,5},{5... | collective-permute-start | bytes 4128776 | tf_op jit(solution)/shard_map/ppermute | solution.py:415
  48.7 61.0 %collective-permute-start.2 = (bf16[2,96,1024]{2,1,0:T(8,128)(2,1)}, bf16[2,96,1024]{2,1,0:T(8,128)(2,1)S(1)}, u32[]{:S(2)}, u32[]{:S(2)}) collective-permute-start(bf16[2,96,1024]{2,1,0:T(8,128)(2,1)} %get-tuple-element.56), channel_id=1, source_target_pairs={{0,6},{1,7},{2,4},{3,5},{4,2},{5,3},{6,0},{7,1},{8,14},{9,15},{10,... | collective-permute-start | bytes 1179656 | tf_op jit(solution)/shard_map/ppermute | solution.py:1089
  109.7 0.8 copy-start
  198.3 55.5 %collective-permute-start.3 = (bf16[4,96,1792]{2,1,0:T(8,128)(2,1)}, bf16[4,96,1792]{2,1,0:T(8,128)(2,1)}, u32[]{:S(2)}, u32[]{:S(2)}) collective-permute-start(bf16[4,96,1792]{2,1,0:T(8,128)(2,1)} %get-tuple-element.67), channel_id=1, source_target_pairs={{0,4},{4,0},{8,12},{12,8},{16,20},{20,16},{24,28},{28,24},{1,5},{5... | collective-permute-start | bytes 4128776 | tf_op jit(solution)/shard_map/ppermute | solution.py:415
  199.6 61.4 %collective-permute-start.4 = (bf16[4,96,1792]{2,1,0:T(8,128)(2,1)}, bf16[4,96,1792]{2,1,0:T(8,128)(2,1)}, u32[]{:S(2)}, u32[]{:S(2)}) collective-permute-start(bf16[4,96,1792]{2,1,0:T(8,128)(2,1)} %get-tuple-element.68), channel_id=1, source_target_pairs={{0,2},{1,3},{2,0},{3,1},{4,6},{5,7},{6,4},{7,5},{8,10},{9,11},{10,... | collective-permute-start | bytes 4128776 | tf_op jit(solution)/shard_map/ppermute | solution.py:411
  200.3 60.6 %collective-permute-start.5 = (bf16[4,96,1792]{2,1,0:T(8,128)(2,1)}, bf16[4,96,1792]{2,1,0:T(8,128)(2,1)}, u32[]{:S(2)}, u32[]{:S(2)}) collective-permute-start(bf16[4,96,1792]{2,1,0:T(8,128)(2,1)} %get-tuple-element.69), channel_id=1, source_target_pairs={{0,6},{1,7},{2,4},{3,5},{4,2},{5,3},{6,0},{7,1},{8,14},{9,15},{10,... | collective-permute-start | bytes 4128776 | tf_op jit(solution)/shard_map/ppermute | solution.py:1089
